TPU v7x, 32 devices: a whole 2x2x4 slice. The times are simulated.
32 devices in a mesh: grp: 2 (over x), seq: 8 (over z, y), head: 2 (over core).
Axes of the slice: x: 2, y: 2, z: 4, core: 2. Of those that a mesh axis runs over, the one named last changes fastest.
Arguments:
- queries: bfloat16 [16384, 2048], P(('grp', 'seq'), 'head'), parts along dimension 0, may hold values from -6 to 6
- key_states: bfloat16 [16384, 1024], P(('grp', 'seq'), 'head'), parts along dimension 0, may hold values from -6 to 6
- value_states: bfloat16 [16384, 1024], P(('grp', 'seq'), 'head'), parts along dimension 0, may hold values from -6 to 6
- segment_ids: int32 [16384], P(('grp', 'seq')), parts along dimension 0, may hold values from 0 to 15, as said below
Outputs:
- attended: bfloat16 [16384, 2048], P(('grp', 'seq'), 'head'), parts along dimension 0
There are 2 independent parts, one for each index of `grp`. A program takes and returns all parts, laid end to end along the dimension named above; each array names one. Nothing has to cross between parts.
Inputs may be any that keep to these rules, and one draw needn't show every extreme that they name: `segment_ids`: read in logical order, the ids never fall, start at 0 and name all 16 candidates, each one token or more; the first 1536 and the last 1536 logical tokens each lie within one candidate.
All inputs are finite; a program needn't handle non-finite values.
Results may differ from a plain program's by a relative error of at most 0.008.
Values may be sent and summed in bfloat16 or wider, within the bound.
No kernel may reach another device: no remote copies, remote signals or barrier semaphores. Data moves between devices by JAX's collectives and lax.ppermute only.
A program may use at most 64 MiB of HBM per device.

v0:
```python
import functools
import math

import jax
import jax.numpy as jnp
from jax import lax
from jax.experimental import pallas as pl
from jax.experimental.pallas import tpu as pltpu
from jax.sharding import PartitionSpec as P

HEAD_DIM = 128
GROUPS = 2
HALF = 512
PAIR = 2
TILE = 256

EXP_SCALE = 168.0 ** (-0.5) * math.log2(math.e)
HIDDEN = -1e30

VMEM = pl.BlockSpec(memory_space=pltpu.VMEM)
SMEM = pl.BlockSpec(memory_space=pltpu.SMEM)
ANY = pl.BlockSpec(memory_space=pl.ANY)
HBM = pl.BlockSpec(memory_space=pltpu.HBM)
PARAMS = pltpu.CompilerParams(vmem_limit_bytes=24 << 20)


def dot_nt(a, b):
    return lax.dot_general(
        a, b, (((1,), (1,)), ((), ())), preferred_element_type=jnp.float32
    )


def dot_nn(a, b):
    return lax.dot_general(
        a, b, (((1,), (0,)), ((), ())), preferred_element_type=jnp.float32
    )


def head_cols(head):
    return slice(head * HEAD_DIM, (head + 1) * HEAD_DIM)


def lane_sum(p):
    total = p[:, :HEAD_DIM]
    for c in range(1, p.shape[1] // HEAD_DIM):
        total = total + p[:, head_cols(c)]
    return total


def same_segment(query_seg, key_seg):
    chunks = key_seg.shape[1] // HEAD_DIM
    return jnp.concatenate([query_seg] * chunks, axis=1) == key_seg


def pack_kernel(k, v, ids, f1, f2, fz, b1, b2, sem):
    copies = []
    for role, pieces in enumerate(((f1, f2), (b1, b2))):
        rows = pl.ds(role * HALF, HALF)
        for h, piece in enumerate(pieces):
            cols = pl.ds(h * PAIR * HEAD_DIM, PAIR * HEAD_DIM)
            for part, src in enumerate((k, v)):
                to = pl.ds(part * PAIR * HEAD_DIM, PAIR * HEAD_DIM)
                block = src.at[rows, cols]
                copies.append((block, piece.at[pl.ds(0, HALF), to]))
                if role == 0:
                    copies.append((block, fz.at[pl.ds(h * HALF, HALF), to]))
    copies = [
        pltpu.make_async_copy(src, dst, sem.at[i]) for i, (src, dst) in enumerate(copies)
    ]
    for copy in copies:
        copy.start()
    for role, piece in enumerate((f1, b1)):
        row = ids[:, role * HALF : (role + 1) * HALF].astype(jnp.float32) + 1.0
        row = jnp.broadcast_to(row, (8, HALF)).astype(jnp.bfloat16)
        piece[HALF : HALF + 8, :] = row
        if role == 0:
            fz[2 * HALF : 2 * HALF + 8, :] = row
    for copy in copies:
        copy.wait()


def pack(k, v, ids):
    def shape(rows):
        return jax.ShapeDtypeStruct((rows, HALF), jnp.bfloat16)

    return pl.pallas_call(
        pack_kernel,
        out_shape=(
            shape(HALF + 8),
            shape(HALF),
            shape(2 * HALF + 8),
            shape(HALF + 8),
            shape(HALF),
        ),
        in_specs=[HBM, HBM, VMEM],
        out_specs=[VMEM] * 5,
        scratch_shapes=[pltpu.SemaphoreType.DMA((12,))],
        compiler_params=PARAMS,
        cost_estimate=pl.CostEstimate(
            flops=1 << 20, bytes_accessed=6 << 20, transcendentals=0
        ),
        name="pack",
    )(k, v, ids)


def stacked_queries(q, rows, first_head):
    return jnp.concatenate(
        [q[rows, head_cols(first_head + j)] for j in range(GROUPS)], axis=0
    )


def near_kernel(h, n, idx, q, k, v, sq, ids, zp, za, pa, zm, piece, acc, mx, ls):
    from_partner = idx[0] >= n - 2
    own_seg = ids[...].astype(jnp.float32) + 1.0
    for role in range(2):
        base = role * HALF
        seg_far = zp[2 * HALF : 2 * HALF + 1, :]
        if role == 1:
            seg_far = jnp.where(
                from_partner, pa[HALF : HALF + 1, :], za[HALF : HALF + 1, :]
            )
        seg_far = seg_far.astype(jnp.float32)
        for g in range(PAIR):
            kcol = head_cols(g)
            vcol = head_cols(PAIR + g)
            own = head_cols(PAIR * h + g)
            far_rows = slice(h * HALF, (h + 1) * HALF)
            if role == 0:
                k_far = zp[far_rows, kcol]
                v_far = zp[far_rows, vcol]
            else:
                k_far = jnp.where(from_partner, piece[0:HALF, kcol], zm[0:HALF, kcol])
                v_far = jnp.where(from_partner, piece[0:HALF, vcol], zm[0:HALF, vcol])
            for i in range(HALF // TILE):
                rows = slice(base + i * TILE, base + (i + 1) * TILE)
                q2 = stacked_queries(q, rows, (PAIR * h + g) * GROUPS)
                n_own = (i + 1) * TILE
                s_own = dot_nt(q2, k[base : base + n_own, own])
                s_far = dot_nt(q2, k_far[i * TILE :])
                seg_q = sq[rows, :]
                see_own = same_segment(seg_q, own_seg[:, base : base + n_own])
                see_far = same_segment(seg_q, seg_far[:, i * TILE :])
                r = lax.broadcasted_iota(jnp.int32, see_own.shape, 0) + i * TILE
                c = lax.broadcasted_iota(jnp.int32, see_own.shape, 1)
                see_own = see_own & (c <= r)
                r = lax.broadcasted_iota(jnp.int32, see_far.shape, 0)
                c = lax.broadcasted_iota(jnp.int32, see_far.shape, 1)
                see_far = see_far & (c > r)
                s_own = jnp.where(jnp.concatenate([see_own] * GROUPS, axis=0), s_own, HIDDEN)
                s_far = jnp.where(jnp.concatenate([see_far] * GROUPS, axis=0), s_far, HIDDEN)
                m = jnp.maximum(
                    jnp.max(s_own, axis=-1, keepdims=True),
                    jnp.max(s_far, axis=-1, keepdims=True),
                )
                p_own = jnp.exp2((s_own - m) * EXP_SCALE)
                p_far = jnp.exp2((s_far - m) * EXP_SCALE)
                part = lane_sum(p_own) + lane_sum(p_far)
                o = dot_nn(p_own.astype(jnp.bfloat16), v[base : base + n_own, own])
                o = o + dot_nn(p_far.astype(jnp.bfloat16), v_far[i * TILE :])
                m = jnp.broadcast_to(m, part.shape)
                for j in range(GROUPS):
                    col = head_cols(GROUPS * g + j)
                    mine = slice(j * TILE, (j + 1) * TILE)
                    acc[rows, col] = o[mine]
                    mx[rows, col] = m[mine]
                    ls[rows, col] = part[mine]


def near(h, n, idx, q, k, v, sq, ids, zp, za, pa, zm, piece):
    state = jax.ShapeDtypeStruct((2 * HALF, 2 * PAIR * HEAD_DIM), jnp.float32)
    return pl.pallas_call(
        functools.partial(near_kernel, h, n),
        out_shape=(state,) * 3,
        in_specs=[SMEM] + [VMEM] * 10,
        out_specs=[VMEM] * 3,
        compiler_params=PARAMS,
        cost_estimate=pl.CostEstimate(
            flops=3 << 30, bytes_accessed=12 << 20, transcendentals=3 << 20
        ),
    )(idx, q, k, v, sq, ids, zp, za, pa, zm, piece)


def last_kernel(h, role, n, idx, q, sq, alt_a, alt_b, alt_seg, kv, kv_seg, acc, mx, ls, *rest):
    out, o_buf, sem = rest[-3:]
    base = role * HALF
    if role == 0:
        use_alt = idx[0] % 2 == 1
        seg = jnp.where(use_alt, alt_seg[HALF : HALF + 1, :], kv_seg[HALF : HALF + 1, :])
        seg = seg.astype(jnp.float32)
    else:
        use_alt = idx[0] == n - 1
        seg = jnp.where(
            use_alt,
            alt_seg[:, 0:HALF].astype(jnp.float32) + 1.0,
            kv_seg[HALF : HALF + 1, :].astype(jnp.float32),
        )
    for g in range(PAIR):
        if role == 0:
            k_alt = alt_a[0:HALF, head_cols(g)]
            v_alt = alt_a[0:HALF, head_cols(PAIR + g)]
        else:
            k_alt = alt_a[0:HALF, head_cols(PAIR * h + g)]
            v_alt = alt_b[0:HALF, head_cols(PAIR * h + g)]
        k_mid = jnp.where(use_alt, k_alt, kv[0:HALF, head_cols(g)])
        v_mid = jnp.where(use_alt, v_alt, kv[0:HALF, head_cols(PAIR + g)])
        for i in range(HALF // TILE):
            rows = slice(base + i * TILE, base + (i + 1) * TILE)
            q2 = stacked_queries(q, rows, (PAIR * h + g) * GROUPS)
            s = dot_nt(q2, k_mid)
            see = same_segment(sq[rows, :], seg)
            s = jnp.where(jnp.concatenate([see] * GROUPS, axis=0), s, HIDDEN)
            cols = [head_cols(GROUPS * g + j) for j in range(GROUPS)]
            m_old = jnp.concatenate([mx[rows, c] for c in cols], axis=0)
            l_old = jnp.concatenate([ls[rows, c] for c in cols], axis=0)
            a_old = jnp.concatenate([acc[rows, c] for c in cols], axis=0)
            m = jnp.maximum(m_old, jnp.max(s, axis=-1, keepdims=True))
            keep = jnp.exp2((m_old - m) * EXP_SCALE)
            p = jnp.exp2((s - jnp.concatenate([m] * (HALF // HEAD_DIM), axis=1)) * EXP_SCALE)
            total = jnp.sum(keep * l_old + lane_sum(p), axis=-1, keepdims=True)
            o = keep * a_old + dot_nn(p.astype(jnp.bfloat16), v_mid)
            o = (o * (1.0 / total)).astype(jnp.bfloat16)
            for j in range(GROUPS):
                o_buf[i * TILE : (i + 1) * TILE, cols[j]] = o[j * TILE : (j + 1) * TILE]
    width = 2 * PAIR * HEAD_DIM
    copy = pltpu.make_async_copy(
        o_buf, out.at[pl.ds(base, HALF), pl.ds(h * width, width)], sem
    )
    copy.start()
    copy.wait()


def last(h, role, n, idx, q, sq, alt_a, alt_b, alt_seg, kv, kv_seg, state, out):
    args = (idx, q, sq, alt_a, alt_b, alt_seg, kv, kv_seg) + state
    aliases = {}
    specs = [SMEM] + [VMEM] * (len(args) - 1)
    if out is not None:
        aliases = {len(args): 0}
        args = args + (out,)
        specs.append(ANY)
    return pl.pallas_call(
        functools.partial(last_kernel, h, role, n),
        out_shape=jax.ShapeDtypeStruct(q.shape, q.dtype),
        in_specs=specs,
        out_specs=ANY,
        input_output_aliases=aliases,
        scratch_shapes=[
            pltpu.VMEM((HALF, 2 * PAIR * HEAD_DIM), jnp.bfloat16),
            pltpu.SemaphoreType.DMA,
        ],
        compiler_params=PARAMS,
        cost_estimate=pl.CostEstimate(
            flops=1 << 30, bytes_accessed=5 << 20, transcendentals=1 << 20
        ),
    )(*args)


def body(queries, key_states, value_states, segment_ids):
    n = lax.axis_size("seq")
    seq = lax.axis_index("seq").astype(jnp.int32)
    idx = seq.reshape(1)
    ids = segment_ids.reshape(1, 2 * HALF)
    sq = jnp.broadcast_to(segment_ids.astype(jnp.float32)[:, None] + 1.0, (2 * HALF, HEAD_DIM))

    partner = [(i, i ^ 1) for i in range(n)]
    up_two = [(i, i + 2) for i in range(n - 2)]
    down_two = [(i + 2, i) for i in range(n - 2)]
    relay = [(i, i + 2) for i in range(0, n - 2, 2)]

    def send(x, route):
        return lax.ppermute(x, "seq", route)

    f1, f2, fz, b1, b2 = pack(
        pltpu.with_memory_space_constraint(key_states, pltpu.HBM),
        pltpu.with_memory_space_constraint(value_states, pltpu.HBM),
        ids,
    )
    pa = send(f1, partner)
    zp = send(fz, up_two)
    za = send(b1, down_two)
    pb = send(f2, partner)
    zb = send(b2, down_two)
    r1 = send(pa, relay)
    even = seq % 2 == 0
    back = jnp.where(even, za, b1)
    d1 = send(back, partner)
    r2 = send(pb, relay)
    back = jnp.where(even, zb, b2)
    d2 = send(back, partner)

    q, k, v = queries, key_states, value_states
    state1 = tuple(near(0, n, idx, q, k, v, sq, ids, zp, za, pa, za, pa))
    state2 = tuple(near(1, n, idx, q, k, v, sq, ids, zp, za, pa, zb, pb))
    out = last(0, 0, n, idx, q, sq, pa, pa, pa, r1, r1, state1, None)
    out = last(0, 1, n, idx, q, sq, k, v, ids, d1, d1, state1, out)
    out = last(1, 1, n, idx, q, sq, k, v, ids, d2, d1, state2, out)
    out = last(1, 0, n, idx, q, sq, pb, pb, pa, r2, r1, state2, out)
    return out


def solution(mesh):
    in_specs = (
        P(("grp", "seq"), "head"),
        P(("grp", "seq"), "head"),
        P(("grp", "seq"), "head"),
        P(("grp", "seq")),
    )
    out_specs = P(("grp", "seq"), "head")
    return jax.shard_map(body, mesh=mesh, in_specs=in_specs, out_specs=out_specs, check_vma=False)
```

profile of v0, /device:TPU:0, one launch (start us, length us, event | category | flops | bytes accessed | tf_op | source)
XLA Modules:
  0.0 74.1 jit_solution(15750573419926482647)
XLA Ops:
  0.0 0.7 copy-done.4
  0.7 3.6 %pack.1 = (bf16[520,512]{1,0:T(8,128)(2,1)}, bf16[512,512]{1,0:T(8,128)(2,1)}, bf16[1032,512]{1,0:T(8,128)(2,1)}, bf16[520,512]{1,0:T(8,128)(2,1)}, bf16[512,512]{1,0:T(8,128)(2,1)}) custom-call(bf16[1024,512]{1,0:T(8,128)(2,1)} %alt_a.3, bf16[1024,512]{1,0:T(8,128)(2,1)} %alt_b.3, s32[1,1024]{1,0:T(1,128)S(1)} %bitcast.2), custom_call_target="tpu_custom_call" | custom-call | flops 1048576 | bytes 6291456 | tf_op jit(solution)/shard_map/pack/pallas_call | solution.py:86
  4.3 0.0 copy-start
  4.3 0.0 copy-start.1
  4.3 0.0 copy-start.5
  4.3 6.2 %collective-permute-start.4 = (bf16[1032,512]{1,0:T(8,128)(2,1)}, bf16[1032,512]{1,0:T(8,128)(2,1)}, u32[]{:S(2)}, u32[]{:S(2)}) collective-permute-start(bf16[1032,512]{1,0:T(8,128)(2,1)} %get-tuple-element.18), channel_id=1, source_target_pairs={{0,4},{2,6},{4,8},{6,10},{8,12},{10,14},{1,5},{3,7},{5,9},{7,11},{... | collective-permute-start | bytes 3170312 | tf_op jit(solution)/shard_map/ppermute | solution.py:270
  10.6 1.3 %collective-permute-start.6 = (bf16[512,512]{1,0:T(8,128)(2,1)}, bf16[512,512]{1,0:T(8,128)(2,1)}, u32[]{:S(2)}, u32[]{:S(2)}) collective-permute-start(bf16[512,512]{1,0:T(8,128)(2,1)} %get-tuple-element.20), channel_id=1, source_target_pairs={{4,0},{6,2},{8,4},{10,6},{12,8},{14,10},{5,1},{7,3},{9,5},{11,7},{... | collective-permute-start | bytes 1572872 | tf_op jit(solution)/shard_map/ppermute | solution.py:270
  11.9 1.3 %collective-permute-start.5 = (bf16[520,512]{1,0:T(8,128)(2,1)}, bf16[520,512]{1,0:T(8,128)(2,1)}, u32[]{:S(2)}, u32[]{:S(2)}) collective-permute-start(bf16[520,512]{1,0:T(8,128)(2,1)} %get-tuple-element.19), channel_id=1, source_target_pairs={{4,0},{6,2},{8,4},{10,6},{12,8},{14,10},{5,1},{7,3},{9,5},{11,7},{... | collective-permute-start | bytes 1597448 | tf_op jit(solution)/shard_map/ppermute | solution.py:270
  13.2 1.6 %collective-permute-start = (bf16[512,512]{1,0:T(8,128)(2,1)}, bf16[512,512]{1,0:T(8,128)(2,1)}, u32[]{:S(2)}, u32[]{:S(2)}) collective-permute-start(bf16[512,512]{1,0:T(8,128)(2,1)} %get-tuple-element.16), channel_id=1, source_target_pairs={{0,2},{2,0},{4,6},{6,4},{8,10},{10,8},{12,14},{14,12},{1,3},{3,1},... | collective-permute-start | bytes 1572872 | tf_op jit(solution)/shard_map/ppermute | solution.py:270
  14.7 0.5 collective-permute-start.1
  15.2 12.3 %collective-permute-done.6.zm = bf16[512,512]{1,0:T(8,128)(2,1)} collective-permute-done((bf16[512,512]{1,0:T(8,128)(2,1)}, bf16[512,512]{1,0:T(8,128)(2,1)}, u32[]{:S(2)}, u32[]{:S(2)}) %collective-permute-start.6) | collective-permute-done | bytes 524320 | tf_op jit(solution)/shard_map/ppermute | solution.py:270
  27.6 1.1 %broadcast_select_fusion.1 = bf16[512,512]{1,0:T(8,128)(2,1)S(1)} fusion(bf16[512,512]{1,0:T(8,128)(2,1)} %collective-permute-done.6.zm, bf16[512,512]{1,0:T(8,128)(2,1)} %get-tuple-element.20, pred[]{:T(512)S(6)} %eq.5), kind=kLoop, calls=%fused_computation.1 | loop fusion | flops 262144 | bytes 1572865 | tf_op jit(solution)/shard_map/jit(_where)/select_n | solution.py:287
  28.7 1.6 %collective-permute-start.7 = (bf16[512,512]{1,0:T(8,128)(2,1)S(1)}, bf16[512,512]{1,0:T(8,128)(2,1)S(1)}, u32[]{:S(2)}, u32[]{:S(2)}) collective-permute-start(bf16[512,512]{1,0:T(8,128)(2,1)S(1)} %broadcast_select_fusion.1), channel_id=1, source_target_pairs={{0,2},{2,0},{4,6},{6,4},{8,10},{10,8},{12,14},{14,12},{1,3},{3,1},... | collective-permute-start | bytes 1572872 | tf_op jit(solution)/shard_map/ppermute | solution.py:270
  30.2 0.0 collective-permute-done.piece.alt_a.alt_b
  30.2 3.3 %collective-permute-start.2 = (bf16[512,512]{1,0:T(8,128)(2,1)}, bf16[512,512]{1,0:T(8,128)(2,1)S(1)}, u32[]{:S(2)}, u32[]{:S(2)}) collective-permute-start(bf16[512,512]{1,0:T(8,128)(2,1)} %collective-permute-done.piece.alt_a.alt_b), channel_id=1, source_target_pairs={{0,4},{4,8},{8,12},{1,5},{5,9},{9,13},{16,20},{20,24},{24,28},{17,... | collective-permute-start | bytes 1572872 | tf_op jit(solution)/shard_map/ppermute | solution.py:270
  33.5 4.0 %collective-permute-done.5.za.zm = bf16[520,512]{1,0:T(8,128)(2,1)} collective-permute-done((bf16[520,512]{1,0:T(8,128)(2,1)}, bf16[520,512]{1,0:T(8,128)(2,1)}, u32[]{:S(2)}, u32[]{:S(2)}) %collective-permute-start.5) | collective-permute-done | bytes 532512 | tf_op jit(solution)/shard_map/ppermute | solution.py:270
  37.6 1.1 %broadcast_select_fusion = bf16[520,512]{1,0:T(8,128)(2,1)S(1)} fusion(bf16[520,512]{1,0:T(8,128)(2,1)} %collective-permute-done.5.za.zm, bf16[520,512]{1,0:T(8,128)(2,1)} %get-tuple-element.19, pred[]{:T(512)S(6)} %eq.5), kind=kLoop, calls=%fused_computation | loop fusion | flops 266240 | bytes 1597441 | tf_op jit(solution)/shard_map/jit(_where)/select_n | solution.py:284
  38.7 1.6 %collective-permute-start.8 = (bf16[520,512]{1,0:T(8,128)(2,1)S(1)}, bf16[520,512]{1,0:T(8,128)(2,1)S(1)}, u32[]{:S(2)}, u32[]{:S(2)}) collective-permute-start(bf16[520,512]{1,0:T(8,128)(2,1)S(1)} %broadcast_select_fusion), channel_id=1, source_target_pairs={{0,2},{2,0},{4,6},{6,4},{8,10},{10,8},{12,14},{14,12},{1,3},{3,1},... | collective-permute-start | bytes 1597448 | tf_op jit(solution)/shard_map/ppermute | solution.py:270
  40.2 0.0 collective-permute-done.1.pa.piece.alt_a.alt_b.alt_seg
  40.2 4.7 %collective-permute-start.3 = (bf16[520,512]{1,0:T(8,128)(2,1)}, bf16[520,512]{1,0:T(8,128)(2,1)S(1)}, u32[]{:S(2)}, u32[]{:S(2)}) collective-permute-start(bf16[520,512]{1,0:T(8,128)(2,1)} %collective-permute-done.1.pa.piece.alt_a.alt_b.alt_seg), channel_id=1, source_target_pairs={{0,4},{4,8},{8,12},{1,5},{5,9},{9,13},{16,20},{20,24},{24,28},{17,... | collective-permute-start | bytes 1597448 | tf_op jit(solution)/shard_map/ppermute | solution.py:270
  44.9 0.0 collective-permute-done.4.zp
  45.0 0.2 broadcast_in_dim.2.sq
  45.2 0.0 copy-start.2
  45.2 1.2 %copy-done.2 = bf16[1024,512]{1,0:T(8,128)(2,1)S(1)} copy-done((bf16[1024,512]{1,0:T(8,128)(2,1)S(1)}, bf16[1024,512]{1,0:T(8,128)(2,1)}, u32[]{:S(2)}) %copy-start.2) | copy-done | bytes 1048600
  46.4 6.5 %shard_map.47 = (f32[1024,512]{1,0:T(8,128)S(1)}, f32[1024,512]{1,0:T(8,128)S(1)}, f32[1024,512]{1,0:T(8,128)S(1)}) custom-call(s32[1]{0:T(128)} %bitcast.idx, bf16[1024,1024]{1,0:T(8,128)(2,1)S(1)} %copy-done, bf16[1024,512]{1,0:T(8,128)(2,1)S(1)} %copy-done.1, bf16[1024,512]{1,0:T(8,128)(2,1)S(1)} %copy-done.2, f32[1024,128]{1,0:T(8,128)S(1)} %broadcast_in_dim.2.sq, ...), custom_call_target="tpu_custom_call" | custom-call | flops 3221225472 | bytes 12582912 | tf_op jit(solution)/shard_map/pallas_call | solution.py:171
  53.0 6.5 %shard_map.46 = (f32[1024,512]{1,0:T(8,128)S(1)}, f32[1024,512]{1,0:T(8,128)S(1)}, f32[1024,512]{1,0:T(8,128)S(1)}) custom-call(s32[1]{0:T(128)} %bitcast.idx, bf16[1024,1024]{1,0:T(8,128)(2,1)S(1)} %copy-done, bf16[1024,512]{1,0:T(8,128)(2,1)S(1)} %copy-done.1, bf16[1024,512]{1,0:T(8,128)(2,1)S(1)} %copy-done.3, f32[1024,128]{1,0:T(8,128)S(1)} %broadcast_in_dim.2.sq, ...), custom_call_target="tpu_custom_call" | custom-call | flops 3221225472 | bytes 12582912 | tf_op jit(solution)/shard_map/pallas_call | solution.py:171
  59.4 0.0 collective-permute-done.3.kv.kv_seg
  59.5 4.3 %shard_map.48.rest_0_ = bf16[1024,1024]{1,0:T(8,128)(2,1)} custom-call(s32[1]{0:T(128)} %bitcast.idx, bf16[1024,1024]{1,0:T(8,128)(2,1)S(1)} %copy-done, f32[1024,128]{1,0:T(8,128)S(1)} %broadcast_in_dim.2.sq, bf16[520,512]{1,0:T(8,128)(2,1)} %collective-permute-done.1.pa.piece.alt_a.alt_b.alt_seg, ...), custom_call_target="tpu_custom_call" | custom-call | flops 1073741824 | bytes 5242880 | tf_op jit(solution)/shard_map/pallas_call | solution.py:240
  63.7 0.0 collective-permute-done.8.kv.kv_seg
  63.7 3.1 %shard_map.49.rest_0_ = bf16[1024,1024]{1,0:T(8,128)(2,1)} custom-call(s32[1]{0:T(128)} %bitcast.idx, bf16[1024,1024]{1,0:T(8,128)(2,1)S(1)} %copy-done, f32[1024,128]{1,0:T(8,128)S(1)} %broadcast_in_dim.2.sq, bf16[1024,512]{1,0:T(8,128)(2,1)S(1)} %copy-done.1, bf16[1024,512]{1,0:T(8,128)(2,1)S(1)} %copy-done.3, ...), custom_call_target="tpu_custom_call", output_to_operand_aliasing={{}: (11, {})} | custom-call | flops 1073741824 | bytes 5242880 | tf_op jit(solution)/shard_map/pallas_call | solution.py:240
  66.8 2.9 %shard_map.50.rest_0_ = bf16[1024,1024]{1,0:T(8,128)(2,1)} custom-call(s32[1]{0:T(128)} %bitcast.idx, bf16[1024,1024]{1,0:T(8,128)(2,1)S(1)} %copy-done, f32[1024,128]{1,0:T(8,128)S(1)} %broadcast_in_dim.2.sq, bf16[1024,512]{1,0:T(8,128)(2,1)S(1)} %copy-done.1, bf16[1024,512]{1,0:T(8,128)(2,1)S(1)} %copy-done.3, ...), custom_call_target="tpu_custom_call", output_to_operand_aliasing={{}: (11, {})} | custom-call | flops 1073741824 | bytes 5242880 | tf_op jit(solution)/shard_map/pallas_call | solution.py:240
  69.8 4.2 %shard_map.51 = bf16[1024,1024]{1,0:T(8,128)(2,1)} custom-call(s32[1]{0:T(128)} %bitcast.idx, bf16[1024,1024]{1,0:T(8,128)(2,1)S(1)} %copy-done, f32[1024,128]{1,0:T(8,128)S(1)} %broadcast_in_dim.2.sq, bf16[512,512]{1,0:T(8,128)(2,1)} %collective-permute-done.piece.alt_a.alt_b, ...), custom_call_target="tpu_custom_call", output_to_operand_aliasing={{}: (11, {})} | custom-call | flops 1073741824 | bytes 5242880 | tf_op jit(solution)/shard_map/pallas_call | solution.py:240
  (9 shorter events, 0.0 us)
Async XLA Ops:
  0.0 0.7 copy-start.4
  4.3 40.8 %copy-start = (bf16[1024,1024]{1,0:T(8,128)(2,1)S(1)}, bf16[1024,1024]{1,0:T(8,128)(2,1)}, u32[]{:S(2)}) copy-start(bf16[1024,1024]{1,0:T(8,128)(2,1)} %q.11) | copy-start | bytes 6291460
  4.3 40.8 %copy-start.1 = (bf16[1024,512]{1,0:T(8,128)(2,1)S(1)}, bf16[1024,512]{1,0:T(8,128)(2,1)}, u32[]{:S(2)}) copy-start(bf16[1024,512]{1,0:T(8,128)(2,1)} %alt_a.3) | copy-start | bytes 3145732
  4.3 40.8 %copy-start.5 = (s32[1024]{0:T(1024)S(1)}, s32[1024]{0:T(1024)}, u32[]{:S(2)}) copy-start(s32[1024]{0:T(1024)} %param.7) | copy-start | bytes 12292
  4.3 40.6 %collective-permute-start.4 = (bf16[1032,512]{1,0:T(8,128)(2,1)}, bf16[1032,512]{1,0:T(8,128)(2,1)}, u32[]{:S(2)}, u32[]{:S(2)}) collective-permute-start(bf16[1032,512]{1,0:T(8,128)(2,1)} %get-tuple-element.18), channel_id=1, source_target_pairs={{0,4},{2,6},{4,8},{6,10},{8,12},{10,14},{1,5},{3,7},{5,9},{7,11},{... | collective-permute-start | bytes 3170312 | tf_op jit(solution)/shard_map/ppermute | solution.py:270
  10.6 17.0 %collective-permute-start.6 = (bf16[512,512]{1,0:T(8,128)(2,1)}, bf16[512,512]{1,0:T(8,128)(2,1)}, u32[]{:S(2)}, u32[]{:S(2)}) collective-permute-start(bf16[512,512]{1,0:T(8,128)(2,1)} %get-tuple-element.20), channel_id=1, source_target_pairs={{4,0},{6,2},{8,4},{10,6},{12,8},{14,10},{5,1},{7,3},{9,5},{11,7},{... | collective-permute-start | bytes 1572872 | tf_op jit(solution)/shard_map/ppermute | solution.py:270
  11.9 25.7 %collective-permute-start.5 = (bf16[520,512]{1,0:T(8,128)(2,1)}, bf16[520,512]{1,0:T(8,128)(2,1)}, u32[]{:S(2)}, u32[]{:S(2)}) collective-permute-start(bf16[520,512]{1,0:T(8,128)(2,1)} %get-tuple-element.19), channel_id=1, source_target_pairs={{4,0},{6,2},{8,4},{10,6},{12,8},{14,10},{5,1},{7,3},{9,5},{11,7},{... | collective-permute-start | bytes 1597448 | tf_op jit(solution)/shard_map/ppermute | solution.py:270
  13.2 17.1 %collective-permute-start = (bf16[512,512]{1,0:T(8,128)(2,1)}, bf16[512,512]{1,0:T(8,128)(2,1)}, u32[]{:S(2)}, u32[]{:S(2)}) collective-permute-start(bf16[512,512]{1,0:T(8,128)(2,1)} %get-tuple-element.16), channel_id=1, source_target_pairs={{0,2},{2,0},{4,6},{6,4},{8,10},{10,8},{12,14},{14,12},{1,3},{3,1},... | collective-permute-start | bytes 1572872 | tf_op jit(solution)/shard_map/ppermute | solution.py:270
  14.7 25.5 %collective-permute-start.1 = (bf16[520,512]{1,0:T(8,128)(2,1)}, bf16[520,512]{1,0:T(8,128)(2,1)}, u32[]{:S(2)}, u32[]{:S(2)}) collective-permute-start(bf16[520,512]{1,0:T(8,128)(2,1)} %get-tuple-element.17), channel_id=1, source_target_pairs={{0,2},{2,0},{4,6},{6,4},{8,10},{10,8},{12,14},{14,12},{1,3},{3,1},... | collective-permute-start | bytes 1597448 | tf_op jit(solution)/shard_map/ppermute | solution.py:270
  28.7 38.2 %collective-permute-start.7 = (bf16[512,512]{1,0:T(8,128)(2,1)S(1)}, bf16[512,512]{1,0:T(8,128)(2,1)S(1)}, u32[]{:S(2)}, u32[]{:S(2)}) collective-permute-start(bf16[512,512]{1,0:T(8,128)(2,1)S(1)} %broadcast_select_fusion.1), channel_id=1, source_target_pairs={{0,2},{2,0},{4,6},{6,4},{8,10},{10,8},{12,14},{14,12},{1,3},{3,1},... | collective-permute-start | bytes 1572872 | tf_op jit(solution)/shard_map/ppermute | solution.py:270
  30.2 39.5 %collective-permute-start.2 = (bf16[512,512]{1,0:T(8,128)(2,1)}, bf16[512,512]{1,0:T(8,128)(2,1)S(1)}, u32[]{:S(2)}, u32[]{:S(2)}) collective-permute-start(bf16[512,512]{1,0:T(8,128)(2,1)} %collective-permute-done.piece.alt_a.alt_b), channel_id=1, source_target_pairs={{0,4},{4,8},{8,12},{1,5},{5,9},{9,13},{16,20},{20,24},{24,28},{17,... | collective-permute-start | bytes 1572872 | tf_op jit(solution)/shard_map/ppermute | solution.py:270
  38.7 25.1 %collective-permute-start.8 = (bf16[520,512]{1,0:T(8,128)(2,1)S(1)}, bf16[520,512]{1,0:T(8,128)(2,1)S(1)}, u32[]{:S(2)}, u32[]{:S(2)}) collective-permute-start(bf16[520,512]{1,0:T(8,128)(2,1)S(1)} %broadcast_select_fusion), channel_id=1, source_target_pairs={{0,2},{2,0},{4,6},{6,4},{8,10},{10,8},{12,14},{14,12},{1,3},{3,1},... | collective-permute-start | bytes 1597448 | tf_op jit(solution)/shard_map/ppermute | solution.py:270
  40.2 19.2 %collective-permute-start.3 = (bf16[520,512]{1,0:T(8,128)(2,1)}, bf16[520,512]{1,0:T(8,128)(2,1)S(1)}, u32[]{:S(2)}, u32[]{:S(2)}) collective-permute-start(bf16[520,512]{1,0:T(8,128)(2,1)} %collective-permute-done.1.pa.piece.alt_a.alt_b.alt_seg), channel_id=1, source_target_pairs={{0,4},{4,8},{8,12},{1,5},{5,9},{9,13},{16,20},{20,24},{24,28},{17,... | collective-permute-start | bytes 1597448 | tf_op jit(solution)/shard_map/ppermute | solution.py:270
  45.2 1.2 %copy-start.2 = (bf16[1024,512]{1,0:T(8,128)(2,1)S(1)}, bf16[1024,512]{1,0:T(8,128)(2,1)}, u32[]{:S(2)}) copy-start(bf16[1024,512]{1,0:T(8,128)(2,1)} %alt_b.3) | copy-start | bytes 3145732
  46.4 6.6 %copy-start.3 = (bf16[1024,512]{1,0:T(8,128)(2,1)S(1)}, bf16[1024,512]{1,0:T(8,128)(2,1)}, u32[]{:S(2)}) copy-start(bf16[1024,512]{1,0:T(8,128)(2,1)} %alt_b.3) | copy-start | bytes 3145732
where the time goes:
time: 74.6 us; the launch traced here: 74.1 us
  Pallas kernels  31.1 us (42%)
  starting transfers between devices  22 us (29%)
  waiting for transfers between devices  16.3 us (22%)
  other arithmetic  2.21 us (3%)
  local copies, waits for them, and re-layouts  2.12 us (3%)
    ppermute x9, starting transfers between devices, send(): return lax.ppermute(x, 'seq', route)  22 us
    ppermute x9, waiting for transfers between devices, send(): return lax.ppermute(x, 'seq', route)  16.3 us
    pallas_call x4, Pallas kernels, last(): pl.pallas_call(functools.partial(last_kernel, h, role, n), out_shape=jax....  14.4 us
    pallas_call x2, Pallas kernels, near(): pl.pallas_call(functools.partial(near_kernel, h, n), out_shape=(state,) *...  13 us
    pallas_call x1, Pallas kernels, pack(): pl.pallas_call(pack_kernel, out_shape=(shape(HALF + 8), shape(HALF), shap...  3.62 us
    unnamed x12, local copies, waits for them, and re-layouts  1.93 us
  transfers between devices with their start and end apart: 9, of which 2 were waited for; matrix products, arithmetic and copies ran while one was open for 3% of the time, Pallas kernels for 31%

commit v1 on v0

v1 whole, which is shorter than its diff:
```python
import functools
import math

import jax
import jax.numpy as jnp
from jax import lax
from jax.experimental import pallas as pl
from jax.experimental.pallas import tpu as pltpu
from jax.sharding import PartitionSpec as P

HEAD_DIM = 128
GROUPS = 2
HALF = 512
PAIR = 2
TILE = 256

EXP_SCALE = 168.0 ** (-0.5) * math.log2(math.e)
HIDDEN = -1e30
MATCH = 12288.0

VMEM = pl.BlockSpec(memory_space=pltpu.VMEM)
SMEM = pl.BlockSpec(memory_space=pltpu.SMEM)
ANY = pl.BlockSpec(memory_space=pl.ANY)
HBM = pl.BlockSpec(memory_space=pltpu.HBM)
PARAMS = pltpu.CompilerParams(vmem_limit_bytes=24 << 20)


def dot_nt(a, b):
    return lax.dot_general(
        a, b, (((1,), (1,)), ((), ())), preferred_element_type=jnp.float32
    )


def dot_nn(a, b):
    return lax.dot_general(
        a, b, (((1,), (0,)), ((), ())), preferred_element_type=jnp.float32
    )


def head_cols(head):
    return slice(head * HEAD_DIM, (head + 1) * HEAD_DIM)


def pack_kernel(k, v, ids, f1, f2, fz, b1, b2, row8, ids_v, sem):
    get_ids = pltpu.make_async_copy(ids, ids_v, sem.at[12])
    get_ids.start()
    copies = []
    for role, pieces in enumerate(((f1, f2), (b1, b2))):
        rows = pl.ds(role * HALF, HALF)
        for h, piece in enumerate(pieces):
            cols = pl.ds(h * PAIR * HEAD_DIM, PAIR * HEAD_DIM)
            for part, src in enumerate((k, v)):
                to = pl.ds(part * PAIR * HEAD_DIM, PAIR * HEAD_DIM)
                block = src.at[rows, cols]
                copies.append((block, piece.at[pl.ds(0, HALF), to]))
                if role == 0:
                    copies.append((block, fz.at[pl.ds(h * HALF, HALF), to]))
    copies = [
        pltpu.make_async_copy(src, dst, sem.at[i]) for i, (src, dst) in enumerate(copies)
    ]
    for copy in copies:
        copy.start()
    get_ids.wait()
    row = jnp.broadcast_to(ids_v[...].astype(jnp.float32) + 1.0, (8, 2 * HALF))
    row = row.astype(jnp.bfloat16)
    row8[...] = row
    f1[HALF : HALF + 8, :] = row[:, :HALF]
    fz[2 * HALF : 2 * HALF + 8, :] = row[:, :HALF]
    b1[HALF : HALF + 8, :] = row[:, HALF:]
    for copy in copies:
        copy.wait()


def pack(k, v, ids):
    def shape(rows, cols=HALF):
        return jax.ShapeDtypeStruct((rows, cols), jnp.bfloat16)

    return pl.pallas_call(
        pack_kernel,
        out_shape=(
            shape(HALF + 8),
            shape(HALF),
            shape(2 * HALF + 8),
            shape(HALF + 8),
            shape(HALF),
            shape(8, 2 * HALF),
        ),
        in_specs=[HBM, HBM, HBM],
        out_specs=[VMEM] * 6,
        scratch_shapes=[
            pltpu.VMEM((1, 2 * HALF), jnp.int32),
            pltpu.SemaphoreType.DMA((13,)),
        ],
        compiler_params=PARAMS,
        cost_estimate=pl.CostEstimate(
            flops=1 << 20, bytes_accessed=6 << 20, transcendentals=0
        ),
        name="pack",
    )(k, v, ids)


def one_hot_keys(row):
    lane = lax.broadcasted_iota(jnp.int32, (HEAD_DIM, HALF), 0).astype(jnp.float32)
    hot = jnp.where(lane == row.astype(jnp.float32), 1.0, 0.0)
    return hot.T.astype(jnp.bfloat16)


def stacked_queries(q, hot, rows, first_head):
    mark = hot[rows, :] * jnp.bfloat16(MATCH)
    return jnp.concatenate(
        [
            jnp.concatenate([q[rows, head_cols(first_head + j)], mark], axis=1)
            for j in range(GROUPS)
        ],
        axis=0,
    )


def with_ones(v):
    return jnp.concatenate([v, jnp.ones(v.shape, v.dtype)], axis=1)


def near_kernel(
    h, n, idx, q, k, v, hot, zp, za, pa, zm, piece, acc, mx, ls, far, seg, sem
):
    from_partner = idx[0] >= n - 2
    body_rows = pl.ds(0, HALF)
    id_rows = pl.ds(HALF, 8)
    copies = [
        pltpu.make_async_copy(zp.at[pl.ds(2 * HALF, 8)], seg.at[0], sem.at[0]),
        pltpu.make_async_copy(zp.at[pl.ds(h * HALF, HALF)], far.at[0], sem.at[1]),
        pltpu.make_async_copy(za.at[id_rows], seg.at[1], sem.at[2]),
        pltpu.make_async_copy(zm.at[body_rows], far.at[1], sem.at[3]),
    ]
    copies[0].start()
    copies[1].start()

    @pl.when(from_partner)
    def _():
        pltpu.make_async_copy(pa.at[id_rows], seg.at[1], sem.at[2]).start()
        pltpu.make_async_copy(piece.at[body_rows], far.at[1], sem.at[3]).start()

    @pl.when(jnp.logical_not(from_partner))
    def _():
        copies[2].start()
        copies[3].start()

    for role in range(2):
        base = role * HALF
        copies[2 * role].wait()
        hot_far = one_hot_keys(seg[role, 0:1, :])
        copies[2 * role + 1].wait()
        for g in range(PAIR):
            own = head_cols(PAIR * h + g)
            k_far = jnp.concatenate([far[role, :, head_cols(g)], hot_far], axis=1)
            v_far = with_ones(far[role, :, head_cols(PAIR + g)])
            for i in range(HALF // TILE):
                rows = slice(base + i * TILE, base + (i + 1) * TILE)
                q2 = stacked_queries(q, hot, rows, (PAIR * h + g) * GROUPS)
                n_own = (i + 1) * TILE
                seen = slice(base, base + n_own)
                k_own = jnp.concatenate([k[seen, own], hot[seen, :]], axis=1)
                s_own = dot_nt(q2, k_own)
                s_far = dot_nt(q2, k_far[i * TILE :])
                r = lax.broadcasted_iota(jnp.int32, (TILE, TILE), 0)
                c = lax.broadcasted_iota(jnp.int32, (TILE, TILE), 1)
                below = jnp.concatenate([c <= r] * GROUPS, axis=0)
                above = jnp.concatenate([c > r] * GROUPS, axis=0)
                edge = jnp.where(below, s_own[:, n_own - TILE :], HIDDEN)
                if i > 0:
                    edge = jnp.concatenate([s_own[:, : n_own - TILE], edge], axis=1)
                s_own = edge
                edge = jnp.where(above, s_far[:, :TILE], HIDDEN)
                if (i + 1) * TILE < HALF:
                    edge = jnp.concatenate([edge, s_far[:, TILE:]], axis=1)
                s_far = edge
                m = jnp.maximum(
                    jnp.max(s_own, axis=-1, keepdims=True),
                    jnp.max(s_far, axis=-1, keepdims=True),
                )
                p_own = jnp.exp2((s_own - m) * EXP_SCALE).astype(jnp.bfloat16)
                p_far = jnp.exp2((s_far - m) * EXP_SCALE).astype(jnp.bfloat16)
                o = dot_nn(p_own, with_ones(v[seen, own]))
                o = o + dot_nn(p_far, v_far[i * TILE :])
                m = jnp.broadcast_to(m, (GROUPS * TILE, HEAD_DIM))
                for j in range(GROUPS):
                    col = head_cols(GROUPS * g + j)
                    mine = slice(j * TILE, (j + 1) * TILE)
                    acc[rows, col] = o[mine, :HEAD_DIM]
                    mx[rows, col] = m[mine]
                    ls[rows, col] = o[mine, HEAD_DIM:]


def near(h, n, idx, q, k, v, hot, zp, za, pa, zm, piece):
    state = jax.ShapeDtypeStruct((2 * HALF, 2 * PAIR * HEAD_DIM), jnp.float32)
    return pl.pallas_call(
        functools.partial(near_kernel, h, n),
        out_shape=(state,) * 3,
        in_specs=[SMEM] + [VMEM] * 4 + [ANY] * 5,
        out_specs=[VMEM] * 3,
        scratch_shapes=[
            pltpu.VMEM((2, HALF, HALF), jnp.bfloat16),
            pltpu.VMEM((2, 8, HALF), jnp.bfloat16),
            pltpu.SemaphoreType.DMA((4,)),
        ],
        compiler_params=PARAMS,
        cost_estimate=pl.CostEstimate(
            flops=3 << 30, bytes_accessed=12 << 20, transcendentals=3 << 20
        ),
    )(idx, q, k, v, hot, zp, za, pa, zm, piece)


def last_kernel(h, role, n, idx, q, hot, alts, alt_seg, kv, kv_seg, acc, mx, ls, *rest):
    out, mid, seg, o_buf, sem, out_sem = rest[-6:]
    base = role * HALF
    width = PAIR * HEAD_DIM
    body_rows = pl.ds(0, HALF)
    k_mid = mid.at[:, pl.ds(0, width)]
    v_mid = mid.at[:, pl.ds(width, width)]
    copies = [
        pltpu.make_async_copy(kv_seg.at[pl.ds(HALF, 8)], seg, sem.at[0]),
        pltpu.make_async_copy(kv.at[body_rows, pl.ds(0, width)], k_mid, sem.at[1]),
        pltpu.make_async_copy(kv.at[body_rows, pl.ds(width, width)], v_mid, sem.at[2]),
    ]
    if role == 0:
        use_alt = idx[0] % 2 == 1
        (piece,) = alts
        others = (
            alt_seg.at[pl.ds(HALF, 8)],
            piece.at[body_rows, pl.ds(0, width)],
            piece.at[body_rows, pl.ds(width, width)],
        )
    else:
        use_alt = idx[0] == n - 1
        own = pl.ds(h * width, width)
        others = (alt_seg.at[:, body_rows],) + tuple(a.at[body_rows, own] for a in alts)

    @pl.when(use_alt)
    def _():
        for i, (src, dst) in enumerate(zip(others, (seg, k_mid, v_mid))):
            pltpu.make_async_copy(src, dst, sem.at[i]).start()

    @pl.when(jnp.logical_not(use_alt))
    def _():
        for copy in copies:
            copy.start()

    copies[0].wait()
    hot_mid = one_hot_keys(seg[0:1, :])
    copies[1].wait()
    sends = []
    for g in range(PAIR):
        k_aug = jnp.concatenate([mid[:, head_cols(g)], hot_mid], axis=1)
        for i in range(HALF // TILE):
            rows = slice(base + i * TILE, base + (i + 1) * TILE)
            q2 = stacked_queries(q, hot, rows, (PAIR * h + g) * GROUPS)
            s = dot_nt(q2, k_aug)
            if g == 0 and i == 0:
                copies[2].wait()
            v_aug = with_ones(mid[:, head_cols(PAIR + g)])
            cols = [head_cols(GROUPS * g + j) for j in range(GROUPS)]
            m_old = jnp.concatenate([mx[rows, c] for c in cols], axis=0)
            l_old = jnp.concatenate([ls[rows, c] for c in cols], axis=0)
            a_old = jnp.concatenate([acc[rows, c] for c in cols], axis=0)
            m = jnp.maximum(m_old, jnp.max(s, axis=-1, keepdims=True))
            keep = jnp.exp2((m_old - m) * EXP_SCALE)
            p = jnp.exp2((s - jnp.concatenate([m] * (HALF // HEAD_DIM), axis=1)) * EXP_SCALE)
            o = dot_nn(p.astype(jnp.bfloat16), v_aug)
            total = keep * l_old + o[:, HEAD_DIM:]
            o = (keep * a_old + o[:, :HEAD_DIM]) * (1.0 / total)
            o = o.astype(jnp.bfloat16)
            for j in range(GROUPS):
                o_buf[i * TILE : (i + 1) * TILE, cols[j]] = o[j * TILE : (j + 1) * TILE]
        part = pl.ds(g * GROUPS * HEAD_DIM, GROUPS * HEAD_DIM)
        to = pl.ds((PAIR * h + g) * GROUPS * HEAD_DIM, GROUPS * HEAD_DIM)
        sends.append(
            pltpu.make_async_copy(
                o_buf.at[:, part], out.at[pl.ds(base, HALF), to], out_sem.at[g]
            )
        )
        sends[-1].start()
    for copy in sends:
        copy.wait()


def last(h, role, n, idx, q, hot, alts, alt_seg, kv, kv_seg, state, out):
    n_alt = len(alts)

    def kernel(idx, q, hot, *refs):
        last_kernel(h, role, n, idx, q, hot, refs[:n_alt], *refs[n_alt:])

    args = (idx, q, hot) + alts + (alt_seg, kv, kv_seg) + state
    specs = [SMEM] + [VMEM] * 2 + [ANY] * (n_alt + 3) + [VMEM] * 3
    aliases = {}
    if out is not None:
        aliases = {len(args): 0}
        args = args + (out,)
        specs.append(ANY)
    return pl.pallas_call(
        kernel,
        out_shape=jax.ShapeDtypeStruct(q.shape, q.dtype),
        in_specs=specs,
        out_specs=ANY,
        input_output_aliases=aliases,
        scratch_shapes=[
            pltpu.VMEM((HALF, HALF), jnp.bfloat16),
            pltpu.VMEM((8, HALF), jnp.bfloat16),
            pltpu.VMEM((HALF, 2 * PAIR * HEAD_DIM), jnp.bfloat16),
            pltpu.SemaphoreType.DMA((3,)),
            pltpu.SemaphoreType.DMA((PAIR,)),
        ],
        compiler_params=PARAMS,
        cost_estimate=pl.CostEstimate(
            flops=1 << 30, bytes_accessed=5 << 20, transcendentals=1 << 20
        ),
    )(*args)


def body(queries, key_states, value_states, segment_ids):
    n = lax.axis_size("seq")
    seq = lax.axis_index("seq").astype(jnp.int32)
    idx = seq.reshape(1)
    lane = jnp.arange(HEAD_DIM, dtype=jnp.int32)
    hot = (segment_ids[:, None] + 1 == lane[None, :]).astype(jnp.bfloat16)

    partner = [(i, i ^ 1) for i in range(n)]
    up_two = [(i, i + 2) for i in range(n - 2)]
    down_two = [(i + 2, i) for i in range(n - 2)]
    relay = [(i, i + 2) for i in range(0, n - 2, 2)]

    def send(x, route):
        return lax.ppermute(x, "seq", route)

    q, k, v = queries, key_states, value_states
    f1, f2, fz, b1, b2, row8 = pack(
        pltpu.with_memory_space_constraint(k, pltpu.HBM),
        pltpu.with_memory_space_constraint(v, pltpu.HBM),
        segment_ids.reshape(1, 2 * HALF),
    )
    pa = send(f1, partner)
    zp = send(fz, up_two)
    za = send(b1, down_two)
    pb = send(f2, partner)
    zb = send(b2, down_two)
    r1 = send(pa, relay)
    even = seq % 2 == 0
    back = jnp.where(even, za, b1)
    d1 = send(back, partner)
    r2 = send(pb, relay)
    back = jnp.where(even, zb, b2)
    d2 = send(back, partner)

    state1 = tuple(near(0, n, idx, q, k, v, hot, zp, za, pa, za, pa))
    state2 = tuple(near(1, n, idx, q, k, v, hot, zp, za, pa, zb, pb))
    out = last(0, 0, n, idx, q, hot, (pa,), pa, r1, r1, state1, None)
    out = last(0, 1, n, idx, q, hot, (k, v), row8, d1, d1, state1, out)
    out = last(1, 1, n, idx, q, hot, (k, v), row8, d2, d1, state2, out)
    out = last(1, 0, n, idx, q, hot, (pb,), pa, r2, r1, state2, out)
    return out


def solution(mesh):
    in_specs = (
        P(("grp", "seq"), "head"),
        P(("grp", "seq"), "head"),
        P(("grp", "seq"), "head"),
        P(("grp", "seq")),
    )
    out_specs = P(("grp", "seq"), "head")
    return jax.shard_map(body, mesh=mesh, in_specs=in_specs, out_specs=out_specs, check_vma=False)
```

time: 74.6 us -> 75.6 us (1.013)
  waiting for transfers between devices: 16.3 us -> 22.6 us
  Pallas kernels: 31.1 us -> 28.2 us
  starting transfers between devices: 22 us -> 19.7 us
    ppermute x9, waiting for transfers between devices: 16.3 us -> 22.6 us  [send(): return lax.ppermute(x, 'seq', route)]
    ppermute x9, starting transfers between devices: 22 us -> 19.7 us  [send(): return lax.ppermute(x, 'seq', route)]
    pallas_call x4, Pallas kernels: 14.4 us -> 12.3 us  [last(): pl.pallas_call(kernel, out_shape=jax.ShapeDtypeStruct(q.shape, q.dtype),...]
    unnamed x12 -> x10, local copies, waits for them, and re-layouts: 1.93 us -> 1.92 us
  transfers between devices with their start and end apart: 9 -> 9, of which waited for: 2 -> 3; matrix products, arithmetic and copies ran while one was open for 3% -> 3% of each run, Pallas kernels for 31% -> 29%
where the time goes in v1:
time: 75.6 us; the launch traced here: 75.2 us
  Pallas kernels  28.2 us (37%)
  waiting for transfers between devices  22.6 us (30%)
  starting transfers between devices  19.7 us (26%)
  other arithmetic  2.42 us (3%)
  local copies, waits for them, and re-layouts  1.92 us (3%)
    ppermute x9, waiting for transfers between devices, send(): return lax.ppermute(x, 'seq', route)  22.6 us
    ppermute x9, starting transfers between devices, send(): return lax.ppermute(x, 'seq', route)  19.7 us
    pallas_call x2, Pallas kernels, near(): pl.pallas_call(functools.partial(near_kernel, h, n), out_shape=(state,) *...  12.4 us
    pallas_call x4, Pallas kernels, last(): pl.pallas_call(kernel, out_shape=jax.ShapeDtypeStruct(q.shape, q.dtype),...  12.3 us
    pallas_call x1, Pallas kernels, pack(): pl.pallas_call(pack_kernel, out_shape=(shape(HALF + 8), shape(HALF), shap...  3.61 us
    unnamed x10, local copies, waits for them, and re-layouts  1.92 us
  transfers between devices with their start and end apart: 9, of which 3 were waited for; matrix products, arithmetic and copies ran while one was open for 3% of the time, Pallas kernels for 29%

profile of v1, /device:TPU:0, one launch (start us, length us, event | category | flops | bytes accessed | tf_op | source)
XLA Modules:
  0.0 75.2 jit_solution(7444907780229896508)
XLA Ops:
  0.0 0.7 copy-done.4
  0.7 3.6 %pack.1 = (bf16[520,512]{1,0:T(8,128)(2,1)}, bf16[512,512]{1,0:T(8,128)(2,1)}, bf16[1032,512]{1,0:T(8,128)(2,1)}, bf16[520,512]{1,0:T(8,128)(2,1)}, bf16[512,512...) custom-call(bf16[1024,512]{1,0:T(8,128)(2,1)} %refs_0_.3, bf16[1024,512]{1,0:T(8,128)(2,1)} %refs_1_.3, s32[1,1024]{1,0:T(1,128)S(1)} %bitcast.2), custom_call_target="tpu_custom_call" | custom-call | flops 1048576 | bytes 6291456 | tf_op jit(solution)/shard_map/pack/pallas_call | solution.py:78
  4.3 0.0 copy-start
  4.3 0.0 copy-start.1
  4.3 6.2 %collective-permute-start.4 = (bf16[1032,512]{1,0:T(8,128)(2,1)}, bf16[1032,512]{1,0:T(8,128)(2,1)}, u32[]{:S(2)}, u32[]{:S(2)}) collective-permute-start(bf16[1032,512]{1,0:T(8,128)(2,1)} %get-tuple-element.19), channel_id=1, source_target_pairs={{0,4},{2,6},{4,8},{6,10},{8,12},{10,14},{1,5},{3,7},{5,9},{7,11},{... | collective-permute-start | bytes 3170312 | tf_op jit(solution)/shard_map/ppermute | solution.py:332
  10.6 1.3 %collective-permute-start.6 = (bf16[512,512]{1,0:T(8,128)(2,1)}, bf16[512,512]{1,0:T(8,128)(2,1)}, u32[]{:S(2)}, u32[]{:S(2)}) collective-permute-start(bf16[512,512]{1,0:T(8,128)(2,1)} %get-tuple-element.21), channel_id=1, source_target_pairs={{4,0},{6,2},{8,4},{10,6},{12,8},{14,10},{5,1},{7,3},{9,5},{11,7},{... | collective-permute-start | bytes 1572872 | tf_op jit(solution)/shard_map/ppermute | solution.py:332
  11.8 1.6 %collective-permute-start.1 = (bf16[520,512]{1,0:T(8,128)(2,1)}, bf16[520,512]{1,0:T(8,128)(2,1)}, u32[]{:S(2)}, u32[]{:S(2)}) collective-permute-start(bf16[520,512]{1,0:T(8,128)(2,1)} %get-tuple-element.18), channel_id=1, source_target_pairs={{0,2},{2,0},{4,6},{6,4},{8,10},{10,8},{12,14},{14,12},{1,3},{3,1},... | collective-permute-start | bytes 1597448 | tf_op jit(solution)/shard_map/ppermute | solution.py:332
  13.4 1.3 %collective-permute-start.5 = (bf16[520,512]{1,0:T(8,128)(2,1)}, bf16[520,512]{1,0:T(8,128)(2,1)}, u32[]{:S(2)}, u32[]{:S(2)}) collective-permute-start(bf16[520,512]{1,0:T(8,128)(2,1)} %get-tuple-element.20), channel_id=1, source_target_pairs={{4,0},{6,2},{8,4},{10,6},{12,8},{14,10},{5,1},{7,3},{9,5},{11,7},{... | collective-permute-start | bytes 1597448 | tf_op jit(solution)/shard_map/ppermute | solution.py:332
  14.7 0.6 collective-permute-start
  15.3 0.2 fusion.hot
  15.5 12.0 %collective-permute-done.6.zm = bf16[512,512]{1,0:T(8,128)(2,1)} collective-permute-done((bf16[512,512]{1,0:T(8,128)(2,1)}, bf16[512,512]{1,0:T(8,128)(2,1)}, u32[]{:S(2)}, u32[]{:S(2)}) %collective-permute-start.6) | collective-permute-done | bytes 524320 | tf_op jit(solution)/shard_map/ppermute | solution.py:332
  27.5 1.1 %broadcast_select_fusion.1 = bf16[512,512]{1,0:T(8,128)(2,1)S(1)} fusion(bf16[512,512]{1,0:T(8,128)(2,1)} %collective-permute-done.6.zm, bf16[512,512]{1,0:T(8,128)(2,1)} %get-tuple-element.21, pred[]{:T(512)S(6)} %eq.21), kind=kLoop, calls=%fused_computation.3 | loop fusion | flops 262144 | bytes 1572865 | tf_op jit(solution)/shard_map/jit(_where)/select_n | solution.py:350
  28.7 1.6 %collective-permute-start.7 = (bf16[512,512]{1,0:T(8,128)(2,1)S(1)}, bf16[512,512]{1,0:T(8,128)(2,1)S(1)}, u32[]{:S(2)}, u32[]{:S(2)}) collective-permute-start(bf16[512,512]{1,0:T(8,128)(2,1)S(1)} %broadcast_select_fusion.1), channel_id=1, source_target_pairs={{0,2},{2,0},{4,6},{6,4},{8,10},{10,8},{12,14},{14,12},{1,3},{3,1},... | collective-permute-start | bytes 1572872 | tf_op jit(solution)/shard_map/ppermute | solution.py:332
  30.2 8.2 %collective-permute-done.piece.refs_0_ = bf16[512,512]{1,0:T(8,128)(2,1)} collective-permute-done((bf16[512,512]{1,0:T(8,128)(2,1)}, bf16[512,512]{1,0:T(8,128)(2,1)}, u32[]{:S(2)}, u32[]{:S(2)}) %collective-permute-start) | collective-permute-done | bytes 524320 | tf_op jit(solution)/shard_map/ppermute | solution.py:332
  38.4 4.6 %collective-permute-start.2 = (bf16[512,512]{1,0:T(8,128)(2,1)}, bf16[512,512]{1,0:T(8,128)(2,1)S(1)}, u32[]{:S(2)}, u32[]{:S(2)}) collective-permute-start(bf16[512,512]{1,0:T(8,128)(2,1)} %collective-permute-done.piece.refs_0_), channel_id=1, source_target_pairs={{0,4},{4,8},{8,12},{1,5},{5,9},{9,13},{16,20},{20,24},{24,28},{17,... | collective-permute-start | bytes 1572872 | tf_op jit(solution)/shard_map/ppermute | solution.py:332
  43.0 0.0 collective-permute-done.5.za.zm
  43.0 1.1 %broadcast_select_fusion = bf16[520,512]{1,0:T(8,128)(2,1)S(1)} fusion(bf16[520,512]{1,0:T(8,128)(2,1)} %collective-permute-done.5.za.zm, bf16[520,512]{1,0:T(8,128)(2,1)} %get-tuple-element.20, pred[]{:T(512)S(6)} %eq.21), kind=kLoop, calls=%fused_computation | loop fusion | flops 266240 | bytes 1597441 | tf_op jit(solution)/shard_map/jit(_where)/select_n | solution.py:347
  44.1 0.1 collective-permute-start.8
  44.2 0.0 collective-permute-done.1.pa.piece.refs_0_.refs_1_
  44.2 2.5 %collective-permute-start.3 = (bf16[520,512]{1,0:T(8,128)(2,1)}, bf16[520,512]{1,0:T(8,128)(2,1)S(1)}, u32[]{:S(2)}, u32[]{:S(2)}) collective-permute-start(bf16[520,512]{1,0:T(8,128)(2,1)} %collective-permute-done.1.pa.piece.refs_0_.refs_1_), channel_id=1, source_target_pairs={{0,4},{4,8},{8,12},{1,5},{5,9},{9,13},{16,20},{20,24},{24,28},{17,... | collective-permute-start | bytes 1597448 | tf_op jit(solution)/shard_map/ppermute | solution.py:332
  46.7 0.0 collective-permute-done.4.zp
  46.8 0.0 copy-start.2
  46.8 1.2 %copy-done.2 = bf16[1024,512]{1,0:T(8,128)(2,1)S(1)} copy-done((bf16[1024,512]{1,0:T(8,128)(2,1)S(1)}, bf16[1024,512]{1,0:T(8,128)(2,1)}, u32[]{:S(2)}) %copy-start.2) | copy-done | bytes 1048600
  48.0 6.2 %shard_map.47 = (f32[1024,512]{1,0:T(8,128)S(1)}, f32[1024,512]{1,0:T(8,128)S(1)}, f32[1024,512]{1,0:T(8,128)S(1)}) custom-call(s32[1]{0:T(128)} %bitcast.idx, bf16[1024,1024]{1,0:T(8,128)(2,1)S(1)} %copy-done, bf16[1024,512]{1,0:T(8,128)(2,1)S(1)} %copy-done.1, bf16[1024,512]{1,0:T(8,128)(2,1)S(1)} %copy-done.2, bf16[1024,128]{1,0:T(8,128)(2,1)S(1)} %fusion.hot, ...), custom_call_target="tpu_custom_call" | custom-call | flops 3221225472 | bytes 12582912 | tf_op jit(solution)/shard_map/pallas_call | solution.py:196
  54.2 6.2 %shard_map.46 = (f32[1024,512]{1,0:T(8,128)S(1)}, f32[1024,512]{1,0:T(8,128)S(1)}, f32[1024,512]{1,0:T(8,128)S(1)}) custom-call(s32[1]{0:T(128)} %bitcast.idx, bf16[1024,1024]{1,0:T(8,128)(2,1)S(1)} %copy-done, bf16[1024,512]{1,0:T(8,128)(2,1)S(1)} %copy-done.1, bf16[1024,512]{1,0:T(8,128)(2,1)S(1)} %copy-done.2, bf16[1024,128]{1,0:T(8,128)(2,1)S(1)} %fusion.hot, ...), custom_call_target="tpu_custom_call" | custom-call | flops 3221225472 | bytes 12582912 | tf_op jit(solution)/shard_map/pallas_call | solution.py:196
  60.4 2.4 %collective-permute-done.3.refs_2_.refs_3_ = bf16[520,512]{1,0:T(8,128)(2,1)S(1)} collective-permute-done((bf16[520,512]{1,0:T(8,128)(2,1)}, bf16[520,512]{1,0:T(8,128)(2,1)S(1)}, u32[]{:S(2)}, u32[]{:S(2)}) %collective-permute-start.3) | collective-permute-done | bytes 532512 | tf_op jit(solution)/shard_map/ppermute | solution.py:332
  62.8 3.2 %shard_map.48.refs_8_ = bf16[1024,1024]{1,0:T(8,128)(2,1)} custom-call(s32[1]{0:T(128)} %bitcast.idx, bf16[1024,1024]{1,0:T(8,128)(2,1)S(1)} %copy-done, bf16[1024,128]{1,0:T(8,128)(2,1)S(1)} %fusion.hot, bf16[520,512]{1,0:T(8,128)(2,1)} %collective-permute-done.1.pa.piece.refs_0_.refs_1_, bf16[520,512]{1,0:T(8,128)(2,1)} %collective-permute-done.1.pa.piece.refs_0_.refs_1_, ...), custom_call_target="tpu_custom_call" | custom-call | flops 1073741824 | bytes 5242880 | tf_op jit(solution)/shard_map/pallas_call | solution.py:299
  65.9 0.0 collective-permute-done.8.refs_3_.refs_4_
  66.0 3.0 %shard_map.49.refs_8_ = bf16[1024,1024]{1,0:T(8,128)(2,1)} custom-call(s32[1]{0:T(128)} %bitcast.idx, bf16[1024,1024]{1,0:T(8,128)(2,1)S(1)} %copy-done, bf16[1024,128]{1,0:T(8,128)(2,1)S(1)} %fusion.hot, bf16[1024,512]{1,0:T(8,128)(2,1)S(1)} %copy-done.1, bf16[1024,512]{1,0:T(8,128)(2,1)S(1)} %copy-done.3, ...), custom_call_target="tpu_custom_call", output_to_operand_aliasing={{}: (11, {})} | custom-call | flops 1073741824 | bytes 5242880 | tf_op jit(solution)/shard_map/pallas_call | solution.py:299
  69.0 0.0 collective-permute-done.7.refs_3_
  69.0 3.0 %shard_map.50.refs_7_ = bf16[1024,1024]{1,0:T(8,128)(2,1)} custom-call(s32[1]{0:T(128)} %bitcast.idx, bf16[1024,1024]{1,0:T(8,128)(2,1)S(1)} %copy-done, bf16[1024,128]{1,0:T(8,128)(2,1)S(1)} %fusion.hot, bf16[1024,512]{1,0:T(8,128)(2,1)S(1)} %copy-done.1, bf16[1024,512]{1,0:T(8,128)(2,1)S(1)} %copy-done.3, ...), custom_call_target="tpu_custom_call", output_to_operand_aliasing={{}: (11, {})} | custom-call | flops 1073741824 | bytes 5242880 | tf_op jit(solution)/shard_map/pallas_call | solution.py:299
  72.0 3.0 %shard_map.51 = bf16[1024,1024]{1,0:T(8,128)(2,1)} custom-call(s32[1]{0:T(128)} %bitcast.idx, bf16[1024,1024]{1,0:T(8,128)(2,1)S(1)} %copy-done, bf16[1024,128]{1,0:T(8,128)(2,1)S(1)} %fusion.hot, bf16[512,512]{1,0:T(8,128)(2,1)} %collective-permute-done.piece.refs_0_, ...), custom_call_target="tpu_custom_call", output_to_operand_aliasing={{}: (10, {})} | custom-call | flops 1073741824 | bytes 5242880 | tf_op jit(solution)/shard_map/pallas_call | solution.py:299
  (7 shorter events, 0.0 us)
Async XLA Ops:
  0.0 0.7 copy-start.4
  4.3 42.4 %copy-start = (bf16[1024,1024]{1,0:T(8,128)(2,1)S(1)}, bf16[1024,1024]{1,0:T(8,128)(2,1)}, u32[]{:S(2)}) copy-start(bf16[1024,1024]{1,0:T(8,128)(2,1)} %q.11) | copy-start | bytes 6291460
  4.3 42.4 %copy-start.1 = (bf16[1024,512]{1,0:T(8,128)(2,1)S(1)}, bf16[1024,512]{1,0:T(8,128)(2,1)}, u32[]{:S(2)}) copy-start(bf16[1024,512]{1,0:T(8,128)(2,1)} %refs_0_.3) | copy-start | bytes 3145732
  4.3 42.4 %collective-permute-start.4 = (bf16[1032,512]{1,0:T(8,128)(2,1)}, bf16[1032,512]{1,0:T(8,128)(2,1)}, u32[]{:S(2)}, u32[]{:S(2)}) collective-permute-start(bf16[1032,512]{1,0:T(8,128)(2,1)} %get-tuple-element.19), channel_id=1, source_target_pairs={{0,4},{2,6},{4,8},{6,10},{8,12},{10,14},{1,5},{3,7},{5,9},{7,11},{... | collective-permute-start | bytes 3170312 | tf_op jit(solution)/shard_map/ppermute | solution.py:332
  10.6 17.0 %collective-permute-start.6 = (bf16[512,512]{1,0:T(8,128)(2,1)}, bf16[512,512]{1,0:T(8,128)(2,1)}, u32[]{:S(2)}, u32[]{:S(2)}) collective-permute-start(bf16[512,512]{1,0:T(8,128)(2,1)} %get-tuple-element.21), channel_id=1, source_target_pairs={{4,0},{6,2},{8,4},{10,6},{12,8},{14,10},{5,1},{7,3},{9,5},{11,7},{... | collective-permute-start | bytes 1572872 | tf_op jit(solution)/shard_map/ppermute | solution.py:332
  11.8 32.4 %collective-permute-start.1 = (bf16[520,512]{1,0:T(8,128)(2,1)}, bf16[520,512]{1,0:T(8,128)(2,1)}, u32[]{:S(2)}, u32[]{:S(2)}) collective-permute-start(bf16[520,512]{1,0:T(8,128)(2,1)} %get-tuple-element.18), channel_id=1, source_target_pairs={{0,2},{2,0},{4,6},{6,4},{8,10},{10,8},{12,14},{14,12},{1,3},{3,1},... | collective-permute-start | bytes 1597448 | tf_op jit(solution)/shard_map/ppermute | solution.py:332
  13.4 29.6 %collective-permute-start.5 = (bf16[520,512]{1,0:T(8,128)(2,1)}, bf16[520,512]{1,0:T(8,128)(2,1)}, u32[]{:S(2)}, u32[]{:S(2)}) collective-permute-start(bf16[520,512]{1,0:T(8,128)(2,1)} %get-tuple-element.20), channel_id=1, source_target_pairs={{4,0},{6,2},{8,4},{10,6},{12,8},{14,10},{5,1},{7,3},{9,5},{11,7},{... | collective-permute-start | bytes 1597448 | tf_op jit(solution)/shard_map/ppermute | solution.py:332
  14.7 23.7 %collective-permute-start = (bf16[512,512]{1,0:T(8,128)(2,1)}, bf16[512,512]{1,0:T(8,128)(2,1)}, u32[]{:S(2)}, u32[]{:S(2)}) collective-permute-start(bf16[512,512]{1,0:T(8,128)(2,1)} %get-tuple-element.17), channel_id=1, source_target_pairs={{0,2},{2,0},{4,6},{6,4},{8,10},{10,8},{12,14},{14,12},{1,3},{3,1},... | collective-permute-start | bytes 1572872 | tf_op jit(solution)/shard_map/ppermute | solution.py:332
  28.7 40.3 %collective-permute-start.7 = (bf16[512,512]{1,0:T(8,128)(2,1)S(1)}, bf16[512,512]{1,0:T(8,128)(2,1)S(1)}, u32[]{:S(2)}, u32[]{:S(2)}) collective-permute-start(bf16[512,512]{1,0:T(8,128)(2,1)S(1)} %broadcast_select_fusion.1), channel_id=1, source_target_pairs={{0,2},{2,0},{4,6},{6,4},{8,10},{10,8},{12,14},{14,12},{1,3},{3,1},... | collective-permute-start | bytes 1572872 | tf_op jit(solution)/shard_map/ppermute | solution.py:332
  38.4 33.6 %collective-permute-start.2 = (bf16[512,512]{1,0:T(8,128)(2,1)}, bf16[512,512]{1,0:T(8,128)(2,1)S(1)}, u32[]{:S(2)}, u32[]{:S(2)}) collective-permute-start(bf16[512,512]{1,0:T(8,128)(2,1)} %collective-permute-done.piece.refs_0_), channel_id=1, source_target_pairs={{0,4},{4,8},{8,12},{1,5},{5,9},{9,13},{16,20},{20,24},{24,28},{17,... | collective-permute-start | bytes 1572872 | tf_op jit(solution)/shard_map/ppermute | solution.py:332
  44.1 21.8 %collective-permute-start.8 = (bf16[520,512]{1,0:T(8,128)(2,1)S(1)}, bf16[520,512]{1,0:T(8,128)(2,1)S(1)}, u32[]{:S(2)}, u32[]{:S(2)}) collective-permute-start(bf16[520,512]{1,0:T(8,128)(2,1)S(1)} %broadcast_select_fusion), channel_id=1, source_target_pairs={{0,2},{2,0},{4,6},{6,4},{8,10},{10,8},{12,14},{14,12},{1,3},{3,1},... | collective-permute-start | bytes 1597448 | tf_op jit(solution)/shard_map/ppermute | solution.py:332
  44.2 18.5 %collective-permute-start.3 = (bf16[520,512]{1,0:T(8,128)(2,1)}, bf16[520,512]{1,0:T(8,128)(2,1)S(1)}, u32[]{:S(2)}, u32[]{:S(2)}) collective-permute-start(bf16[520,512]{1,0:T(8,128)(2,1)} %collective-permute-done.1.pa.piece.refs_0_.refs_1_), channel_id=1, source_target_pairs={{0,4},{4,8},{8,12},{1,5},{5,9},{9,13},{16,20},{20,24},{24,28},{17,... | collective-permute-start | bytes 1597448 | tf_op jit(solution)/shard_map/ppermute | solution.py:332
  46.8 1.2 %copy-start.2 = (bf16[1024,512]{1,0:T(8,128)(2,1)S(1)}, bf16[1024,512]{1,0:T(8,128)(2,1)}, u32[]{:S(2)}) copy-start(bf16[1024,512]{1,0:T(8,128)(2,1)} %refs_1_.3) | copy-start | bytes 3145732
  62.8 3.2 %copy-start.3 = (bf16[1024,512]{1,0:T(8,128)(2,1)S(1)}, bf16[1024,512]{1,0:T(8,128)(2,1)}, u32[]{:S(2)}) copy-start(bf16[1024,512]{1,0:T(8,128)(2,1)} %refs_1_.3) | copy-start | bytes 3145732

commit v2 on v1

v2 whole, which is shorter than its diff:
```python
import functools
import math

import jax
import jax.numpy as jnp
from jax import lax
from jax.experimental import pallas as pl
from jax.experimental.pallas import tpu as pltpu
from jax.sharding import PartitionSpec as P

HEAD_DIM = 128
GROUPS = 2
HALF = 512
PAIR = 2
TILE = 256
TILES = HALF // TILE

EXP_SCALE = 168.0 ** (-0.5) * math.log2(math.e)
HIDDEN = -1e30
MATCH = 12288.0

VMEM = pl.BlockSpec(memory_space=pltpu.VMEM)
SMEM = pl.BlockSpec(memory_space=pltpu.SMEM)
ANY = pl.BlockSpec(memory_space=pl.ANY)
HBM = pl.BlockSpec(memory_space=pltpu.HBM)
PARAMS = pltpu.CompilerParams(vmem_limit_bytes=24 << 20)


def dot_nt(a, b):
    return lax.dot_general(
        a, b, (((1,), (1,)), ((), ())), preferred_element_type=jnp.float32
    )


def dot_nn(a, b):
    return lax.dot_general(
        a, b, (((1,), (0,)), ((), ())), preferred_element_type=jnp.float32
    )


def head_cols(head):
    return slice(head * HEAD_DIM, (head + 1) * HEAD_DIM)


def pack_kernel(k, v, ids, f1, f2, fz, b1, b2, row8, ids_v, sem):
    get_ids = pltpu.make_async_copy(ids, ids_v, sem.at[12])
    get_ids.start()
    copies = []
    for role, pieces in enumerate(((f1, f2), (b1, b2))):
        rows = pl.ds(role * HALF, HALF)
        for h, piece in enumerate(pieces):
            cols = pl.ds(h * PAIR * HEAD_DIM, PAIR * HEAD_DIM)
            for part, src in enumerate((k, v)):
                to = pl.ds(part * PAIR * HEAD_DIM, PAIR * HEAD_DIM)
                block = src.at[rows, cols]
                copies.append((block, piece.at[pl.ds(0, HALF), to]))
                if role == 0:
                    copies.append((block, fz.at[pl.ds(h * HALF, HALF), to]))
    copies = [
        pltpu.make_async_copy(src, dst, sem.at[i]) for i, (src, dst) in enumerate(copies)
    ]
    for copy in copies:
        copy.start()
    get_ids.wait()
    row = jnp.broadcast_to(ids_v[...].astype(jnp.float32) + 1.0, (8, 2 * HALF))
    row = row.astype(jnp.bfloat16)
    row8[...] = row
    f1[HALF : HALF + 8, :] = row[:, :HALF]
    fz[2 * HALF : 2 * HALF + 8, :] = row[:, :HALF]
    b1[HALF : HALF + 8, :] = row[:, HALF:]
    for copy in copies:
        copy.wait()


def pack(k, v, ids):
    def shape(rows, cols=HALF):
        return jax.ShapeDtypeStruct((rows, cols), jnp.bfloat16)

    return pl.pallas_call(
        pack_kernel,
        out_shape=(
            shape(HALF + 8),
            shape(HALF),
            shape(2 * HALF + 8),
            shape(HALF + 8),
            shape(HALF),
            shape(8, 2 * HALF),
        ),
        in_specs=[HBM, HBM, HBM],
        out_specs=[VMEM] * 6,
        scratch_shapes=[
            pltpu.VMEM((1, 2 * HALF), jnp.int32),
            pltpu.SemaphoreType.DMA((13,)),
        ],
        compiler_params=PARAMS,
        cost_estimate=pl.CostEstimate(
            flops=1 << 20, bytes_accessed=6 << 20, transcendentals=0
        ),
        name="pack",
    )(k, v, ids)


def one_hot_keys(row):
    lane = lax.broadcasted_iota(jnp.int32, (HEAD_DIM, HALF), 0).astype(jnp.float32)
    hot = jnp.where(lane == row.astype(jnp.float32), 1.0, 0.0)
    return hot.T.astype(jnp.bfloat16)


def stacked_queries(q, hot, base, first_head):
    blocks = []
    for i in range(TILES):
        rows = slice(base + i * TILE, base + (i + 1) * TILE)
        mark = hot[rows, :] * jnp.bfloat16(MATCH)
        for j in range(GROUPS):
            blocks.append(jnp.concatenate([q[rows, head_cols(first_head + j)], mark], axis=1))
    return jnp.concatenate(blocks, axis=0)


def with_ones(v):
    return jnp.concatenate([v, jnp.ones(v.shape, v.dtype)], axis=1)


def tile_rows(x, i):
    return x[i * GROUPS * TILE : (i + 1) * GROUPS * TILE]


def edge_mask(above):
    r = lax.broadcasted_iota(jnp.int32, (TILE, TILE), 0)
    c = lax.broadcasted_iota(jnp.int32, (TILE, TILE), 1)
    return jnp.concatenate([c > r if above else c <= r] * GROUPS, axis=0)


def triangle_scores(q2, k_aug, above):
    mask = edge_mask(above)
    seen = [[] for _ in range(TILES)]
    for t in range(TILES):
        first, end = (0, t + 1) if above else (t, TILES)
        rows = q2[first * GROUPS * TILE : end * GROUPS * TILE]
        s = dot_nt(rows, k_aug[t * TILE : (t + 1) * TILE])
        for i in range(first, end):
            part = tile_rows(s, i - first)
            if i == t:
                part = jnp.where(mask, part, HIDDEN)
            seen[i].append(part)
    return seen


def triangle_values(probs, v_aug, above):
    total = [None] * TILES
    for t in range(TILES):
        first, end = (0, t + 1) if above else (t, TILES)
        rows = jnp.concatenate(
            [probs[i][t - i if above else t] for i in range(first, end)], axis=0
        )
        o = dot_nn(rows, v_aug[t * TILE : (t + 1) * TILE])
        for i in range(first, end):
            part = tile_rows(o, i - first)
            total[i] = part if total[i] is None else total[i] + part
    return total


def row_max(parts):
    top = parts[0]
    for part in parts[1:]:
        top = jnp.maximum(top, part)
    return jnp.max(top, axis=-1, keepdims=True)


def weights(parts, m):
    wide = jnp.concatenate([m] * (TILE // HEAD_DIM), axis=1)
    return [jnp.exp2((part - wide) * EXP_SCALE).astype(jnp.bfloat16) for part in parts]


def state_slices(base, g):
    for i in range(TILES):
        for j in range(GROUPS):
            rows = slice(base + i * TILE, base + (i + 1) * TILE)
            yield i, slice(j * TILE, (j + 1) * TILE), rows, head_cols(GROUPS * g + j)


def load_state(ref, base, g):
    parts = [[] for _ in range(TILES)]
    for i, _, rows, cols in state_slices(base, g):
        parts[i].append(ref[rows, cols])
    return [jnp.concatenate(p, axis=0) for p in parts]


def own_kernel(h, q, k, v, hot, acc, mx, ls):
    for role in range(2):
        base = role * HALF
        seen = slice(base, base + HALF)
        for g in range(PAIR):
            own = head_cols(PAIR * h + g)
            q2 = stacked_queries(q, hot, base, (PAIR * h + g) * GROUPS)
            k_aug = jnp.concatenate([k[seen, own], hot[seen, :]], axis=1)
            scores = triangle_scores(q2, k_aug, False)
            tops = [
                jnp.broadcast_to(row_max(parts), (GROUPS * TILE, HEAD_DIM)) for parts in scores
            ]
            probs = [weights(parts, m) for parts, m in zip(scores, tops)]
            o = triangle_values(probs, with_ones(v[seen, own]), False)
            for i, mine, rows, cols in state_slices(base, g):
                acc[rows, cols] = o[i][mine, :HEAD_DIM]
                ls[rows, cols] = o[i][mine, HEAD_DIM:]
                mx[rows, cols] = tops[i][mine]


STATE = jax.ShapeDtypeStruct((2 * HALF, 2 * PAIR * HEAD_DIM), jnp.float32)


def cost(gflop):
    return pl.CostEstimate(
        flops=gflop << 30, bytes_accessed=8 << 20, transcendentals=2 << 20
    )


def own(h, q, k, v, hot):
    return pl.pallas_call(
        functools.partial(own_kernel, h),
        out_shape=(STATE,) * 3,
        in_specs=[VMEM] * 4,
        out_specs=[VMEM] * 3,
        compiler_params=PARAMS,
        cost_estimate=cost(2),
    )(q, k, v, hot)


def far_kernel(h, n, idx, q, hot, zp, za, pa, zm, piece, acc0, mx0, ls0, acc, mx, ls):
    from_partner = idx[0] >= n - 2
    for role in range(2):
        base = role * HALF
        if role == 0:
            seg = zp[2 * HALF : 2 * HALF + 1, :]
            far = zp[h * HALF : (h + 1) * HALF, :]
        else:
            seg = jnp.where(from_partner, pa[HALF : HALF + 1, :], za[HALF : HALF + 1, :])
            far = jnp.where(from_partner, piece[0:HALF, :], zm[0:HALF, :])
        hot_far = one_hot_keys(seg)
        for g in range(PAIR):
            q2 = stacked_queries(q, hot, base, (PAIR * h + g) * GROUPS)
            k_aug = jnp.concatenate([far[:, head_cols(g)], hot_far], axis=1)
            scores = triangle_scores(q2, k_aug, True)
            old = load_state(mx0, base, g)
            tops = [jnp.maximum(m, row_max(parts)) for m, parts in zip(old, scores)]
            probs = [weights(parts, m) for parts, m in zip(scores, tops)]
            o = triangle_values(probs, with_ones(far[:, head_cols(PAIR + g)]), True)
            for i, mine, rows, cols in state_slices(base, g):
                keep = jnp.exp2((old[i][mine] - tops[i][mine]) * EXP_SCALE)
                acc[rows, cols] = keep * acc0[rows, cols] + o[i][mine, :HEAD_DIM]
                ls[rows, cols] = keep * ls0[rows, cols] + o[i][mine, HEAD_DIM:]
                mx[rows, cols] = tops[i][mine]


def far(h, n, idx, q, hot, zp, za, pa, zm, piece, state):
    return pl.pallas_call(
        functools.partial(far_kernel, h, n),
        out_shape=(STATE,) * 3,
        in_specs=[SMEM] + [VMEM] * 10,
        out_specs=[VMEM] * 3,
        compiler_params=PARAMS,
        cost_estimate=cost(2),
    )(idx, q, hot, zp, za, pa, zm, piece, *state)


def last_kernel(
    h, n, idx, q, hot, k, v, row8, pa, piece, r1, relayed, d1, back, acc, mx, ls, *rest
):
    out, o_buf, sem = rest[-3:]
    odd = idx[0] % 2 == 1
    end = idx[0] == n - 1
    width = PAIR * HEAD_DIM
    mine_cols = slice(h * width, (h + 1) * width)
    sends = []
    for role in range(2):
        base = role * HALF
        if role == 0:
            seg = jnp.where(odd, pa[HALF : HALF + 1, :], r1[HALF : HALF + 1, :])
            k_mid = jnp.where(odd, piece[0:HALF, :width], relayed[0:HALF, :width])
            v_mid = jnp.where(odd, piece[0:HALF, width:], relayed[0:HALF, width:])
        else:
            seg = jnp.where(end, row8[0:1, :HALF], d1[HALF : HALF + 1, :])
            k_mid = jnp.where(end, k[0:HALF, mine_cols], back[0:HALF, :width])
            v_mid = jnp.where(end, v[0:HALF, mine_cols], back[0:HALF, width:])
        hot_mid = one_hot_keys(seg)
        for g in range(PAIR):
            q2 = stacked_queries(q, hot, base, (PAIR * h + g) * GROUPS)
            k_aug = jnp.concatenate([k_mid[:, head_cols(g)], hot_mid], axis=1)
            s = dot_nt(q2, k_aug)
            old = jnp.concatenate(load_state(mx, base, g), axis=0)
            m = jnp.maximum(old, jnp.max(s, axis=-1, keepdims=True))
            keep = jnp.exp2((old - m) * EXP_SCALE)
            wide = jnp.concatenate([m] * (HALF // HEAD_DIM), axis=1)
            p = jnp.exp2((s - wide) * EXP_SCALE).astype(jnp.bfloat16)
            o = dot_nn(p, with_ones(v_mid[:, head_cols(g)]))
            for i, mine, rows, cols in state_slices(base, g):
                o_i, keep_i = tile_rows(o, i)[mine], tile_rows(keep, i)[mine]
                total = keep_i * ls[rows, cols] + o_i[:, HEAD_DIM:]
                value = keep_i * acc[rows, cols] + o_i[:, :HEAD_DIM]
                o_buf[rows, cols] = (value * (1.0 / total)).astype(jnp.bfloat16)
            part = pl.ds(g * GROUPS * HEAD_DIM, GROUPS * HEAD_DIM)
            to = pl.ds((PAIR * h + g) * GROUPS * HEAD_DIM, GROUPS * HEAD_DIM)
            here = pl.ds(base, HALF)
            sends.append(
                pltpu.make_async_copy(
                    o_buf.at[here, part], out.at[here, to], sem.at[PAIR * role + g]
                )
            )
            sends[-1].start()
    for copy in sends:
        copy.wait()


def last(h, n, idx, q, hot, k, v, row8, pa, piece, r1, relayed, d1, back, state, out):
    args = (idx, q, hot, k, v, row8, pa, piece, r1, relayed, d1, back) + state
    specs = [SMEM] + [VMEM] * (len(args) - 1)
    aliases = {}
    if out is not None:
        aliases = {len(args): 0}
        args = args + (out,)
        specs.append(ANY)
    return pl.pallas_call(
        functools.partial(last_kernel, h, n),
        out_shape=jax.ShapeDtypeStruct(q.shape, q.dtype),
        in_specs=specs,
        out_specs=ANY,
        input_output_aliases=aliases,
        scratch_shapes=[
            pltpu.VMEM((2 * HALF, 2 * PAIR * HEAD_DIM), jnp.bfloat16),
            pltpu.SemaphoreType.DMA((2 * PAIR,)),
        ],
        compiler_params=PARAMS,
        cost_estimate=cost(2),
    )(*args)


def body(queries, key_states, value_states, segment_ids):
    n = lax.axis_size("seq")
    seq = lax.axis_index("seq").astype(jnp.int32)
    idx = seq.reshape(1)
    lane = jnp.arange(HEAD_DIM, dtype=jnp.int32)
    hot = (segment_ids[:, None] + 1 == lane[None, :]).astype(jnp.bfloat16)

    partner = [(i, i ^ 1) for i in range(n)]
    up_two = [(i, i + 2) for i in range(n - 2)]
    down_two = [(i + 2, i) for i in range(n - 2)]
    relay = [(i, i + 2) for i in range(0, n - 2, 2)]

    def send(x, route):
        return lax.ppermute(x, "seq", route)

    q, k, v = queries, key_states, value_states
    f1, f2, fz, b1, b2, row8 = pack(
        pltpu.with_memory_space_constraint(k, pltpu.HBM),
        pltpu.with_memory_space_constraint(v, pltpu.HBM),
        pltpu.with_memory_space_constraint(segment_ids.reshape(1, 2 * HALF), pltpu.HBM),
    )
    pa = send(f1, partner)
    zp = send(fz, up_two)
    za = send(b1, down_two)
    pb = send(f2, partner)
    zb = send(b2, down_two)
    state1 = tuple(own(0, q, k, v, hot))
    r1 = send(pa, relay)
    state2 = tuple(own(1, q, k, v, hot))
    even = seq % 2 == 0
    back = jnp.where(even, za, b1)
    d1 = send(back, partner)
    r2 = send(pb, relay)
    back = jnp.where(even, zb, b2)
    d2 = send(back, partner)

    state1 = tuple(far(0, n, idx, q, hot, zp, za, pa, za, pa, state1))
    state2 = tuple(far(1, n, idx, q, hot, zp, za, pa, zb, pb, state2))
    out = last(0, n, idx, q, hot, k, v, row8, pa, pa, r1, r1, d1, d1, state1, None)
    return last(1, n, idx, q, hot, k, v, row8, pa, pb, r1, r2, d1, d2, state2, out)


def solution(mesh):
    in_specs = (
        P(("grp", "seq"), "head"),
        P(("grp", "seq"), "head"),
        P(("grp", "seq"), "head"),
        P(("grp", "seq")),
    )
    out_specs = P(("grp", "seq"), "head")
    return jax.shard_map(body, mesh=mesh, in_specs=in_specs, out_specs=out_specs, check_vma=False)
```

time: 75.6 us -> 63.8 us (0.84)
  waiting for transfers between devices: 22.6 us -> 4.19 us
  local copies, waits for them, and re-layouts: 1.92 us -> 8.86 us
  starting transfers between devices: 19.7 us -> 21.8 us
  Pallas kernels: 28.2 us -> 26.6 us
  other arithmetic: 2.42 us -> 1.4 us
    ppermute x9, waiting for transfers between devices: 22.6 us -> 4.19 us  [send(): return lax.ppermute(x, 'seq', route)]
    unnamed x10 -> x24, local copies, waits for them, and re-layouts: 1.92 us -> 8.86 us
    ppermute x9, starting transfers between devices: 19.7 us -> 21.8 us  [send(): return lax.ppermute(x, 'seq', route)]
    pallas_call x6, Pallas kernels: 24.6 us -> 22.9 us  [the longest x2 9.84 us: last(): pl.pallas_call(functools.partial(last_kernel, h, n), out_shape=jax.ShapeD...]
    select_n x1, other arithmetic: 1.11 us -> 0.08 us  [body(): back = jnp.where(even, za, b1)]
  transfers between devices with their start and end apart: 9 -> 9, of which waited for: 3 -> 2; matrix products, arithmetic and copies ran while one was open for 3% -> 2% of each run, Pallas kernels for 29% -> 27%
where the time goes in v2:
time: 63.8 us; the launch traced here: 63.3 us
  Pallas kernels  26.6 us (42%)
  starting transfers between devices  21.8 us (34%)
  local copies, waits for them, and re-layouts  8.86 us (14%)
  waiting for transfers between devices  4.19 us (7%)
  other arithmetic  1.4 us (2%)
    ppermute x9, starting transfers between devices, send(): return lax.ppermute(x, 'seq', route)  21.8 us
    pallas_call x2, Pallas kernels, last(): pl.pallas_call(functools.partial(last_kernel, h, n), out_shape=jax.ShapeD...  9.84 us
    unnamed x24, local copies, waits for them, and re-layouts  8.86 us
    pallas_call x2, Pallas kernels, far(): pl.pallas_call(functools.partial(far_kernel, h, n), out_shape=(STATE,) *...  8.5 us
    pallas_call x2, Pallas kernels, own(): pl.pallas_call(functools.partial(own_kernel, h), out_shape=(STATE,) * 3,...  4.51 us
    ppermute x9, waiting for transfers between devices, send(): return lax.ppermute(x, 'seq', route)  4.19 us
    pallas_call x1, Pallas kernels, pack(): pl.pallas_call(pack_kernel, out_shape=(shape(HALF + 8), shape(HALF), shap...  3.77 us
  transfers between devices with their start and end apart: 9, of which 2 were waited for; matrix products, arithmetic and copies ran while one was open for 2% of the time, Pallas kernels for 27%

profile of v2, /device:TPU:0, one launch (start us, length us, event | category | flops | bytes accessed | tf_op | source)
XLA Modules:
  0.0 63.3 jit_solution(17627672669946887233)
XLA Ops:
  0.0 3.8 %pack.1 = (bf16[520,512]{1,0:T(8,128)(2,1)}, bf16[512,512]{1,0:T(8,128)(2,1)}, bf16[1032,512]{1,0:T(8,128)(2,1)}, bf16[520,512]{1,0:T(8,128)(2,1)}, bf16[512,512...) custom-call(bf16[1024,512]{1,0:T(8,128)(2,1)} %k.9, bf16[1024,512]{1,0:T(8,128)(2,1)} %v.9, s32[1,1024]{1,0:T(1,128)} %bitcast.2), custom_call_target="tpu_custom_call" | custom-call | flops 1048576 | bytes 6291456 | tf_op jit(solution)/shard_map/pack/pallas_call | solution.py:79
  3.8 1.3 %collective-permute-start.4 = (bf16[520,512]{1,0:T(8,128)(2,1)}, bf16[520,512]{1,0:T(8,128)(2,1)S(1)}, u32[]{:S(2)}, u32[]{:S(2)}) collective-permute-start(bf16[520,512]{1,0:T(8,128)(2,1)} %get-tuple-element.26), channel_id=1, source_target_pairs={{4,0},{6,2},{8,4},{10,6},{12,8},{14,10},{5,1},{7,3},{9,5},{11,7},{... | collective-permute-start | bytes 1597448 | tf_op jit(solution)/shard_map/ppermute | solution.py:349
  5.1 3.1 %collective-permute-start = (bf16[520,512]{1,0:T(8,128)(2,1)}, bf16[520,512]{1,0:T(8,128)(2,1)S(1)}, u32[]{:S(2)}, u32[]{:S(2)}) collective-permute-start(bf16[520,512]{1,0:T(8,128)(2,1)} %get-tuple-element.24), channel_id=1, source_target_pairs={{0,2},{2,0},{4,6},{6,4},{8,10},{10,8},{12,14},{14,12},{1,3},{3,1},... | collective-permute-start | bytes 1597448 | tf_op jit(solution)/shard_map/ppermute | solution.py:349
  8.1 5.5 %collective-permute-start.8 = (bf16[1032,512]{1,0:T(8,128)(2,1)}, bf16[1032,512]{1,0:T(8,128)(2,1)}, u32[]{:S(2)}, u32[]{:S(2)}) collective-permute-start(bf16[1032,512]{1,0:T(8,128)(2,1)} %get-tuple-element.28), channel_id=1, source_target_pairs={{0,4},{2,6},{4,8},{6,10},{8,12},{10,14},{1,5},{3,7},{5,9},{7,11},{... | collective-permute-start | bytes 3170312 | tf_op jit(solution)/shard_map/ppermute | solution.py:349
  13.7 1.3 %collective-permute-start.6 = (bf16[512,512]{1,0:T(8,128)(2,1)}, bf16[512,512]{1,0:T(8,128)(2,1)}, u32[]{:S(2)}, u32[]{:S(2)}) collective-permute-start(bf16[512,512]{1,0:T(8,128)(2,1)} %get-tuple-element.27), channel_id=1, source_target_pairs={{4,0},{6,2},{8,4},{10,6},{12,8},{14,10},{5,1},{7,3},{9,5},{11,7},{... | collective-permute-start | bytes 1572872 | tf_op jit(solution)/shard_map/ppermute | solution.py:349
  15.0 0.1 collective-permute-start.1
  15.1 0.2 fusion.hot
  15.3 0.0 copy-start.1
  15.4 1.2 %copy-done.1 = bf16[1024,512]{1,0:T(8,128)(2,1)S(1)} copy-done((bf16[1024,512]{1,0:T(8,128)(2,1)S(1)}, bf16[1024,512]{1,0:T(8,128)(2,1)}, u32[]{:S(2)}) %copy-start.1) | copy-done | bytes 1048600
  16.6 1.2 %copy-done.3 = bf16[1024,512]{1,0:T(8,128)(2,1)S(1)} copy-done((bf16[1024,512]{1,0:T(8,128)(2,1)S(1)}, bf16[1024,512]{1,0:T(8,128)(2,1)}, u32[]{:S(2)}) %copy-start.3) | copy-done | bytes 1048600
  17.8 2.2 %shard_map.48 = (f32[1024,512]{1,0:T(8,128)S(1)}, f32[1024,512]{1,0:T(8,128)S(1)}, f32[1024,512]{1,0:T(8,128)S(1)}) custom-call(bf16[1024,1024]{1,0:T(8,128)(2,1)S(1)} %copy-done, bf16[1024,512]{1,0:T(8,128)(2,1)S(1)} %copy-done.1, bf16[1024,512]{1,0:T(8,128)(2,1)S(1)} %copy-done.3, bf16[1024,128]{1,0:T(8,128)(2,1)S(1)} %fusion.hot), custom_call_target="tpu_custom_call" | custom-call | flops 2147483648 | bytes 8388608 | tf_op jit(solution)/shard_map/pallas_call | solution.py:218
  20.0 0.0 copy-start.5
  20.0 1.3 %copy-done.5 = f32[1024,512]{1,0:T(8,128)} copy-done((f32[1024,512]{1,0:T(8,128)}, f32[1024,512]{1,0:T(8,128)S(1)}, u32[]{:S(2)}) %copy-start.5) | copy-done | bytes 2097176
  21.4 1.3 %copy-done.7 = f32[1024,512]{1,0:T(8,128)} copy-done((f32[1024,512]{1,0:T(8,128)}, f32[1024,512]{1,0:T(8,128)S(1)}, u32[]{:S(2)}) %copy-start.7) | copy-done | bytes 2097176
  22.7 1.3 %copy-done.9 = f32[1024,512]{1,0:T(8,128)} copy-done((f32[1024,512]{1,0:T(8,128)}, f32[1024,512]{1,0:T(8,128)S(1)}, u32[]{:S(2)}) %copy-start.9) | copy-done | bytes 2097176
  24.0 1.2 %copy-done.2 = bf16[1024,512]{1,0:T(8,128)(2,1)S(1)} copy-done((bf16[1024,512]{1,0:T(8,128)(2,1)S(1)}, bf16[1024,512]{1,0:T(8,128)(2,1)}, u32[]{:S(2)}) %copy-start.2) | copy-done | bytes 1048600
  25.2 1.2 %copy-done.4 = bf16[1024,512]{1,0:T(8,128)(2,1)S(1)} copy-done((bf16[1024,512]{1,0:T(8,128)(2,1)S(1)}, bf16[1024,512]{1,0:T(8,128)(2,1)}, u32[]{:S(2)}) %copy-start.4) | copy-done | bytes 1048600
  26.4 2.3 %shard_map.46 = (f32[1024,512]{1,0:T(8,128)S(1)}, f32[1024,512]{1,0:T(8,128)S(1)}, f32[1024,512]{1,0:T(8,128)S(1)}) custom-call(bf16[1024,1024]{1,0:T(8,128)(2,1)S(1)} %copy-done, bf16[1024,512]{1,0:T(8,128)(2,1)S(1)} %copy-done.2, bf16[1024,512]{1,0:T(8,128)(2,1)S(1)} %copy-done.4, bf16[1024,128]{1,0:T(8,128)(2,1)S(1)} %fusion.hot), custom_call_target="tpu_custom_call" | custom-call | flops 2147483648 | bytes 8388608 | tf_op jit(solution)/shard_map/pallas_call | solution.py:218
  28.7 0.0 copy-start.6
  28.7 0.1 broadcast_select_fusion
  28.8 3.2 %collective-permute-start.5 = (bf16[520,512]{1,0:T(8,128)(2,1)S(1)}, bf16[520,512]{1,0:T(8,128)(2,1)S(1)}, u32[]{:S(2)}, u32[]{:S(2)}) collective-permute-start(bf16[520,512]{1,0:T(8,128)(2,1)S(1)} %broadcast_select_fusion), channel_id=1, source_target_pairs={{0,2},{2,0},{4,6},{6,4},{8,10},{10,8},{12,14},{14,12},{1,3},{3,1},... | collective-permute-start | bytes 1597448 | tf_op jit(solution)/shard_map/ppermute | solution.py:349
  32.0 0.0 collective-permute-done.pa.piece
  32.0 4.6 %collective-permute-start.2 = (bf16[520,512]{1,0:T(8,128)(2,1)S(1)}, bf16[520,512]{1,0:T(8,128)(2,1)S(1)}, u32[]{:S(2)}, u32[]{:S(2)}) collective-permute-start(bf16[520,512]{1,0:T(8,128)(2,1)S(1)} %collective-permute-done.pa.piece), channel_id=1, source_target_pairs={{0,4},{4,8},{8,12},{1,5},{5,9},{9,13},{16,20},{20,24},{24,28},{17,... | collective-permute-start | bytes 1597448 | tf_op jit(solution)/shard_map/ppermute | solution.py:349
  36.6 1.1 %broadcast_select_fusion.1 = bf16[512,512]{1,0:T(8,128)(2,1)S(1)} fusion(bf16[512,512]{1,0:T(8,128)(2,1)} %collective-permute-done.6.zm, bf16[512,512]{1,0:T(8,128)(2,1)} %get-tuple-element.27, pred[]{:T(512)S(6)} %eq.21), kind=kLoop, calls=%fused_computation.3 | loop fusion | flops 262144 | bytes 1572865 | tf_op jit(solution)/shard_map/jit(_where)/select_n | solution.py:369
  37.7 0.1 collective-permute-start.7
  37.8 2.7 %collective-permute-start.3 = (bf16[512,512]{1,0:T(8,128)(2,1)}, bf16[512,512]{1,0:T(8,128)(2,1)S(1)}, u32[]{:S(2)}, u32[]{:S(2)}) collective-permute-start(bf16[512,512]{1,0:T(8,128)(2,1)} %collective-permute-done.1.piece), channel_id=1, source_target_pairs={{0,4},{4,8},{8,12},{1,5},{5,9},{9,13},{16,20},{20,24},{24,28},{17,... | collective-permute-start | bytes 1572872 | tf_op jit(solution)/shard_map/ppermute | solution.py:349
  40.6 4.1 %shard_map.49 = (f32[1024,512]{1,0:T(8,128)S(1)}, f32[1024,512]{1,0:T(8,128)S(1)}, f32[1024,512]{1,0:T(8,128)S(1)}) custom-call(s32[1]{0:T(128)} %bitcast.idx, bf16[1024,1024]{1,0:T(8,128)(2,1)S(1)} %copy-done, bf16[1024,128]{1,0:T(8,128)(2,1)S(1)} %fusion.hot, bf16[1032,512]{1,0:T(8,128)(2,1)} %collective-permute-done.8.zp, ...), custom_call_target="tpu_custom_call" | custom-call | flops 2147483648 | bytes 8388608 | tf_op jit(solution)/shard_map/pallas_call | solution.py:255
  44.7 4.4 %shard_map.47 = (f32[1024,512]{1,0:T(8,128)S(1)}, f32[1024,512]{1,0:T(8,128)S(1)}, f32[1024,512]{1,0:T(8,128)S(1)}) custom-call(s32[1]{0:T(128)} %bitcast.idx, bf16[1024,1024]{1,0:T(8,128)(2,1)S(1)} %copy-done, bf16[1024,128]{1,0:T(8,128)(2,1)S(1)} %fusion.hot, bf16[1032,512]{1,0:T(8,128)(2,1)} %collective-permute-done.8.zp, ...), custom_call_target="tpu_custom_call" | custom-call | flops 2147483648 | bytes 8388608 | tf_op jit(solution)/shard_map/pallas_call | solution.py:255
  49.1 4.4 %shard_map.50.rest_0_ = bf16[1024,1024]{1,0:T(8,128)(2,1)} custom-call(s32[1]{0:T(128)} %bitcast.idx, bf16[1024,1024]{1,0:T(8,128)(2,1)S(1)} %copy-done, bf16[1024,128]{1,0:T(8,128)(2,1)S(1)} %fusion.hot, bf16[1024,512]{1,0:T(8,128)(2,1)S(1)} %copy-done.2, bf16[1024,512]{1,0:T(8,128)(2,1)S(1)} %copy-done.4, bf16[8,1024]{1,0:T(8,128)(2,1)S(1)} %get-tuple-element.23.row8, ...), custom_call_target="tpu_custom_call" | custom-call | flops 2147483648 | bytes 8388608 | tf_op jit(solution)/shard_map/pallas_call | solution.py:321
  53.5 0.8 %collective-permute-done.7.back = bf16[512,512]{1,0:T(8,128)(2,1)S(1)} collective-permute-done((bf16[512,512]{1,0:T(8,128)(2,1)S(1)}, bf16[512,512]{1,0:T(8,128)(2,1)S(1)}, u32[]{:S(2)}, u32[]{:S(2)}) %collective-permute-start.7) | collective-permute-done | bytes 524320 | tf_op jit(solution)/shard_map/ppermute | solution.py:349
  54.3 3.3 %collective-permute-done.3.relayed = bf16[512,512]{1,0:T(8,128)(2,1)S(1)} collective-permute-done((bf16[512,512]{1,0:T(8,128)(2,1)}, bf16[512,512]{1,0:T(8,128)(2,1)S(1)}, u32[]{:S(2)}, u32[]{:S(2)}) %collective-permute-start.3) | collective-permute-done | bytes 524320 | tf_op jit(solution)/shard_map/ppermute | solution.py:349
  57.7 5.5 %shard_map.51 = bf16[1024,1024]{1,0:T(8,128)(2,1)} custom-call(s32[1]{0:T(128)} %bitcast.idx, bf16[1024,1024]{1,0:T(8,128)(2,1)S(1)} %copy-done, bf16[1024,128]{1,0:T(8,128)(2,1)S(1)} %fusion.hot, bf16[1024,512]{1,0:T(8,128)(2,1)S(1)} %copy-done.2, bf16[1024,512]{1,0:T(8,128)(2,1)S(1)} %copy-done.4, ...), custom_call_target="tpu_custom_call", output_to_operand_aliasing={{}: (15, {})} | custom-call | flops 2147483648 | bytes 8388608 | tf_op jit(solution)/shard_map/pallas_call | solution.py:321
  (21 shorter events, 0.0 us)
Async XLA Ops:
  0.0 15.1 %copy-start.11 = (s32[1024]{0:T(1024)S(1)}, s32[1024]{0:T(1024)}, u32[]{:S(2)}) copy-start(s32[1024]{0:T(1024)} %param.7) | copy-start | bytes 12292
  0.0 15.3 %copy-start = (bf16[1024,1024]{1,0:T(8,128)(2,1)S(1)}, bf16[1024,1024]{1,0:T(8,128)(2,1)}, u32[]{:S(2)}) copy-start(bf16[1024,1024]{1,0:T(8,128)(2,1)} %q.11) | copy-start | bytes 6291460
  3.8 25.0 %collective-permute-start.4 = (bf16[520,512]{1,0:T(8,128)(2,1)}, bf16[520,512]{1,0:T(8,128)(2,1)S(1)}, u32[]{:S(2)}, u32[]{:S(2)}) collective-permute-start(bf16[520,512]{1,0:T(8,128)(2,1)} %get-tuple-element.26), channel_id=1, source_target_pairs={{4,0},{6,2},{8,4},{10,6},{12,8},{14,10},{5,1},{7,3},{9,5},{11,7},{... | collective-permute-start | bytes 1597448 | tf_op jit(solution)/shard_map/ppermute | solution.py:349
  5.1 27.0 %collective-permute-start = (bf16[520,512]{1,0:T(8,128)(2,1)}, bf16[520,512]{1,0:T(8,128)(2,1)S(1)}, u32[]{:S(2)}, u32[]{:S(2)}) collective-permute-start(bf16[520,512]{1,0:T(8,128)(2,1)} %get-tuple-element.24), channel_id=1, source_target_pairs={{0,2},{2,0},{4,6},{6,4},{8,10},{10,8},{12,14},{14,12},{1,3},{3,1},... | collective-permute-start | bytes 1597448 | tf_op jit(solution)/shard_map/ppermute | solution.py:349
  8.1 32.4 %collective-permute-start.8 = (bf16[1032,512]{1,0:T(8,128)(2,1)}, bf16[1032,512]{1,0:T(8,128)(2,1)}, u32[]{:S(2)}, u32[]{:S(2)}) collective-permute-start(bf16[1032,512]{1,0:T(8,128)(2,1)} %get-tuple-element.28), channel_id=1, source_target_pairs={{0,4},{2,6},{4,8},{6,10},{8,12},{10,14},{1,5},{3,7},{5,9},{7,11},{... | collective-permute-start | bytes 3170312 | tf_op jit(solution)/shard_map/ppermute | solution.py:349
  13.7 22.9 %collective-permute-start.6 = (bf16[512,512]{1,0:T(8,128)(2,1)}, bf16[512,512]{1,0:T(8,128)(2,1)}, u32[]{:S(2)}, u32[]{:S(2)}) collective-permute-start(bf16[512,512]{1,0:T(8,128)(2,1)} %get-tuple-element.27), channel_id=1, source_target_pairs={{4,0},{6,2},{8,4},{10,6},{12,8},{14,10},{5,1},{7,3},{9,5},{11,7},{... | collective-permute-start | bytes 1572872 | tf_op jit(solution)/shard_map/ppermute | solution.py:349
  15.0 22.9 %collective-permute-start.1 = (bf16[512,512]{1,0:T(8,128)(2,1)}, bf16[512,512]{1,0:T(8,128)(2,1)}, u32[]{:S(2)}, u32[]{:S(2)}) collective-permute-start(bf16[512,512]{1,0:T(8,128)(2,1)} %get-tuple-element.25), channel_id=1, source_target_pairs={{0,2},{2,0},{4,6},{6,4},{8,10},{10,8},{12,14},{14,12},{1,3},{3,1},... | collective-permute-start | bytes 1572872 | tf_op jit(solution)/shard_map/ppermute | solution.py:349
  15.3 1.2 %copy-start.1 = (bf16[1024,512]{1,0:T(8,128)(2,1)S(1)}, bf16[1024,512]{1,0:T(8,128)(2,1)}, u32[]{:S(2)}) copy-start(bf16[1024,512]{1,0:T(8,128)(2,1)} %k.9) | copy-start | bytes 3145732
  16.6 1.2 %copy-start.3 = (bf16[1024,512]{1,0:T(8,128)(2,1)S(1)}, bf16[1024,512]{1,0:T(8,128)(2,1)}, u32[]{:S(2)}) copy-start(bf16[1024,512]{1,0:T(8,128)(2,1)} %v.9) | copy-start | bytes 3145732
  20.0 1.3 %copy-start.5 = (f32[1024,512]{1,0:T(8,128)}, f32[1024,512]{1,0:T(8,128)S(1)}, u32[]{:S(2)}) copy-start(f32[1024,512]{1,0:T(8,128)S(1)} %get-tuple-element.35.acc0) | copy-start | bytes 6291460
  21.3 1.3 %copy-start.7 = (f32[1024,512]{1,0:T(8,128)}, f32[1024,512]{1,0:T(8,128)S(1)}, u32[]{:S(2)}) copy-start(f32[1024,512]{1,0:T(8,128)S(1)} %get-tuple-element.36.mx0) | copy-start | bytes 6291460
  22.7 1.3 %copy-start.9 = (f32[1024,512]{1,0:T(8,128)}, f32[1024,512]{1,0:T(8,128)S(1)}, u32[]{:S(2)}) copy-start(f32[1024,512]{1,0:T(8,128)S(1)} %get-tuple-element.37.ls0) | copy-start | bytes 6291460
  24.0 1.2 %copy-start.2 = (bf16[1024,512]{1,0:T(8,128)(2,1)S(1)}, bf16[1024,512]{1,0:T(8,128)(2,1)}, u32[]{:S(2)}) copy-start(bf16[1024,512]{1,0:T(8,128)(2,1)} %k.9) | copy-start | bytes 3145732
  25.2 1.2 %copy-start.4 = (bf16[1024,512]{1,0:T(8,128)(2,1)S(1)}, bf16[1024,512]{1,0:T(8,128)(2,1)}, u32[]{:S(2)}) copy-start(bf16[1024,512]{1,0:T(8,128)(2,1)} %v.9) | copy-start | bytes 3145732
  26.4 14.1 %copy-start.8 = (f32[1024,512]{1,0:T(8,128)S(1)}, f32[1024,512]{1,0:T(8,128)}, u32[]{:S(2)}) copy-start(f32[1024,512]{1,0:T(8,128)} %copy-done.7) | copy-start | bytes 6291460
  26.4 14.1 %copy-start.10 = (f32[1024,512]{1,0:T(8,128)S(1)}, f32[1024,512]{1,0:T(8,128)}, u32[]{:S(2)}) copy-start(f32[1024,512]{1,0:T(8,128)} %copy-done.9) | copy-start | bytes 6291460
  28.7 11.8 %copy-start.6 = (f32[1024,512]{1,0:T(8,128)S(1)}, f32[1024,512]{1,0:T(8,128)}, u32[]{:S(2)}) copy-start(f32[1024,512]{1,0:T(8,128)} %copy-done.5) | copy-start | bytes 6291460
  28.8 20.2 %collective-permute-start.5 = (bf16[520,512]{1,0:T(8,128)(2,1)S(1)}, bf16[520,512]{1,0:T(8,128)(2,1)S(1)}, u32[]{:S(2)}, u32[]{:S(2)}) collective-permute-start(bf16[520,512]{1,0:T(8,128)(2,1)S(1)} %broadcast_select_fusion), channel_id=1, source_target_pairs={{0,2},{2,0},{4,6},{6,4},{8,10},{10,8},{12,14},{14,12},{1,3},{3,1},... | collective-permute-start | bytes 1597448 | tf_op jit(solution)/shard_map/ppermute | solution.py:349
  32.0 17.0 %collective-permute-start.2 = (bf16[520,512]{1,0:T(8,128)(2,1)S(1)}, bf16[520,512]{1,0:T(8,128)(2,1)S(1)}, u32[]{:S(2)}, u32[]{:S(2)}) collective-permute-start(bf16[520,512]{1,0:T(8,128)(2,1)S(1)} %collective-permute-done.pa.piece), channel_id=1, source_target_pairs={{0,4},{4,8},{8,12},{1,5},{5,9},{9,13},{16,20},{20,24},{24,28},{17,... | collective-permute-start | bytes 1597448 | tf_op jit(solution)/shard_map/ppermute | solution.py:349
  37.7 16.6 %collective-permute-start.7 = (bf16[512,512]{1,0:T(8,128)(2,1)S(1)}, bf16[512,512]{1,0:T(8,128)(2,1)S(1)}, u32[]{:S(2)}, u32[]{:S(2)}) collective-permute-start(bf16[512,512]{1,0:T(8,128)(2,1)S(1)} %broadcast_select_fusion.1), channel_id=1, source_target_pairs={{0,2},{2,0},{4,6},{6,4},{8,10},{10,8},{12,14},{14,12},{1,3},{3,1},... | collective-permute-start | bytes 1572872 | tf_op jit(solution)/shard_map/ppermute | solution.py:349
  37.8 19.8 %collective-permute-start.3 = (bf16[512,512]{1,0:T(8,128)(2,1)}, bf16[512,512]{1,0:T(8,128)(2,1)S(1)}, u32[]{:S(2)}, u32[]{:S(2)}) collective-permute-start(bf16[512,512]{1,0:T(8,128)(2,1)} %collective-permute-done.1.piece), channel_id=1, source_target_pairs={{0,4},{4,8},{8,12},{1,5},{5,9},{9,13},{16,20},{20,24},{24,28},{17,... | collective-permute-start | bytes 1572872 | tf_op jit(solution)/shard_map/ppermute | solution.py:349
